TPU v7x, 32 devices: a whole 2x2x4 slice. The times are simulated.
32 devices in a mesh: dp: 8 (over z, x), tensor: 4 (over y, core).
Axes of the slice: x: 2, y: 2, z: 4, core: 2. Of those that a mesh axis runs over, the one named last changes fastest.
Arguments:
- tokens: bfloat16 [32, 512, 768], P('dp', 'tensor'), may hold values from -6 to 6
- lengths: int32 [32], P('dp'), may hold values from 64 to 512, as said below
- grad_out: bfloat16 [32, 512, 768], P('dp', 'tensor'), may hold values from -6 to 6
- qkv_weight: bfloat16 [3, 768, 768], P(None, 'dp', 'tensor'), may hold values from -0.21875 to 0.21875
- out_weight: bfloat16 [768, 768], P('tensor', 'dp'), may hold values from -1.25 to 1.25
- up_weight: bfloat16 [768, 3072], P('dp', 'tensor'), may hold values from -0.21875 to 0.21875
- down_weight: bfloat16 [3072, 768], P('tensor', 'dp'), may hold values from -0.109375 to 0.109375
- vectors: bfloat16 [8, 768], P(None, 'dp'), may hold values from -1.6 to 1.6
- hidden_bias: bfloat16 [3072], P('dp'), may hold values from -1.5 to 1.5
Outputs:
- output: bfloat16 [32, 512, 768], P('dp', 'tensor')
- grad_tokens: float32 [32, 512, 768], P('dp', 'tensor')
- query_key_value_gradient: float32 [3, 768, 768], P(None, 'dp', 'tensor')
- grad_out_weight: float32 [768, 768], P('tensor', 'dp')
- grad_up: float32 [768, 3072], P('dp', 'tensor')
- grad_down: float32 [3072, 768], P('tensor', 'dp')
- grad_vectors: float32 [8, 768], P(None, 'dp')
- grad_hidden_bias: float32 [3072], P('dp')
Inputs may be any that keep to these rules, and one draw needn't show every extreme that they name: `lengths`: each sequence's valid tokens; some sequence has all 512 valid in every draw.
All inputs are finite; a program needn't handle non-finite values.
Results may differ from a plain program's by a relative error of at most 0.02.
Values may be sent and summed in bfloat16 or wider, within the bound.
A program may use at most 128 MiB of HBM per device.

v0:
```python
import jax
import jax.numpy as jnp
from jax import lax
from jax.sharding import PartitionSpec as P

HD = 64


def layer_norm(residual, norm_gain, norm_shift):
    mean_row = jnp.mean(residual, axis=-1, keepdims=True)
    centred = residual - mean_row
    spread = jnp.mean(centred * centred, axis=-1, keepdims=True)
    return centred * lax.rsqrt(spread + 1e-12) * norm_gain + norm_shift


def gelu_exact(inputs):
    return jax.nn.gelu(inputs, approximate=False)


def attend_forward(queries, key_rows, values, length):
    seq_len = key_rows.shape[0]
    key_valid = jnp.arange(seq_len) < length
    scores = (
        jnp.einsum("qhe,khe->hqk", queries, key_rows, preferred_element_type=jnp.float32) * 0.125
    )
    scores = jnp.where(key_valid[None, None, :], scores, -1e30)
    highest = jnp.max(scores, axis=-1, keepdims=True)
    exponent = jnp.exp(scores - highest)
    denominator = jnp.sum(exponent, axis=-1, keepdims=True)
    probabilities = (exponent / denominator).astype(jnp.bfloat16)
    attention_context = jnp.einsum(
        "hqk,khe->qhe", probabilities, values, preferred_element_type=jnp.float32
    )
    contexts = [attention_context.astype(jnp.bfloat16)]
    log_parts = [highest + jnp.log(denominator)]
    return (jnp.concatenate(contexts, axis=0), jnp.concatenate(log_parts, axis=1))


def attend_backward(queries, key_rows, values, length, log_sums, grad_context):
    seq_len = key_rows.shape[0]
    block_rows = min(512, seq_len)
    key_valid = jnp.arange(seq_len) < length
    grad_keys = jnp.zeros(key_rows.shape, jnp.float32)
    grad_values = jnp.zeros(values.shape, jnp.float32)
    scores = (
        jnp.einsum("qhe,khe->hqk", queries, key_rows, preferred_element_type=jnp.float32) * 0.125
    )
    scores = jnp.where(key_valid[None, None, :], scores, -1e30)
    probabilities = jnp.exp(scores - log_sums[:, 0:block_rows])
    grad_probs = jnp.einsum(
        "qhe,khe->hqk", grad_context, values, preferred_element_type=jnp.float32
    )
    row_dots = jnp.sum(grad_probs * probabilities, axis=-1, keepdims=True)
    grad_scores = (probabilities * (grad_probs - row_dots)).astype(jnp.bfloat16)
    query_grads = [
        jnp.einsum("hqk,khe->qhe", grad_scores, key_rows, preferred_element_type=jnp.float32)
        * 0.125
    ]
    grad_keys = (
        grad_keys
        + jnp.einsum("hqk,qhe->khe", grad_scores, queries, preferred_element_type=jnp.float32)
        * 0.125
    )
    grad_values = grad_values + jnp.einsum(
        "hqk,qhe->khe",
        probabilities.astype(jnp.bfloat16),
        grad_context,
        preferred_element_type=jnp.float32,
    )
    return (jnp.concatenate(query_grads, axis=0), grad_keys, grad_values)


def shards(
    tokens, lengths, grad_out, qkv_weight, out_weight, up_weight, down_weight, vectors, hidden_bias
):
    tensor_count = lax.axis_size("tensor")
    tensor_rank = lax.axis_index("tensor")
    (
        query_key_value_full,
        output_weight_rows,
        up_weight_columns,
        down_weight_rows,
        vector_all,
        bias_all,
    ) = (
        lax.all_gather(qkv_weight, "dp", axis=1, tiled=True),
        lax.all_gather(out_weight, "dp", axis=1, tiled=True),
        lax.all_gather(up_weight, "dp", axis=0, tiled=True),
        lax.all_gather(down_weight, "dp", axis=1, tiled=True),
        lax.all_gather(vectors, "dp", axis=1, tiled=True),
        lax.all_gather(hidden_bias, "dp", axis=0, tiled=True),
    )
    model_width = query_key_value_full.shape[1]
    local_width = query_key_value_full.shape[2]
    local_hidden = up_weight_columns.shape[1]
    full_hidden = bias_all.shape[0]
    heads_here = local_width // HD
    seqs_here = tokens.shape[0]
    seq_len = tokens.shape[1] * tensor_count
    vector_rows = vector_all.astype(jnp.float32)
    query_bias = lax.dynamic_slice_in_dim(vector_rows[0], tensor_rank * local_width, local_width)
    value_bias = lax.dynamic_slice_in_dim(vector_rows[1], tensor_rank * local_width, local_width)
    unit_bias = lax.dynamic_slice_in_dim(
        bias_all.astype(jnp.float32), tensor_rank * local_hidden, local_hidden
    )
    token_gathered = lax.all_gather(tokens, "tensor", axis=1, tiled=True)
    projected_output = jnp.einsum(
        "hqu,auf->ahqf", token_gathered, query_key_value_full, preferred_element_type=jnp.float32
    )
    head_shape = (seqs_here, seq_len, heads_here, HD)
    queries = (projected_output[0] + query_bias).astype(jnp.bfloat16).reshape(head_shape)
    key_rows = projected_output[1].astype(jnp.bfloat16).reshape(head_shape)
    values = (projected_output[2] + value_bias).astype(jnp.bfloat16).reshape(head_shape)

    def forward_one(operands):
        return attend_forward(operands[0], operands[1], operands[2], operands[3])

    attention_context, log_sums = lax.map(forward_one, (queries, key_rows, values, lengths))
    attention_context = attention_context.reshape(seqs_here, seq_len, local_width)
    attention_portion = jnp.einsum(
        "njb,bz->njz", attention_context, output_weight_rows, preferred_element_type=jnp.float32
    )
    attn_share = lax.psum_scatter(
        attention_portion.astype(jnp.bfloat16), "tensor", scatter_dimension=1, tiled=True
    ).astype(jnp.float32)
    resid_one = tokens.astype(jnp.float32) + attn_share + vector_rows[2]
    hidden = layer_norm(resid_one, vector_rows[3], vector_rows[4])
    hidden_gathered = lax.all_gather(hidden.astype(jnp.bfloat16), "tensor", axis=1, tiled=True)
    pre_act = (
        jnp.einsum(
            "bjr,rv->bjv", hidden_gathered, up_weight_columns, preferred_element_type=jnp.float32
        )
        + unit_bias
    )
    gelu_activations = gelu_exact(pre_act).astype(jnp.bfloat16)
    feedforward_portion = jnp.einsum(
        "yic,cg->yig", gelu_activations, down_weight_rows, preferred_element_type=jnp.float32
    )
    ffn_share = lax.psum_scatter(
        feedforward_portion.astype(jnp.bfloat16), "tensor", scatter_dimension=1, tiled=True
    ).astype(jnp.float32)
    resid_two = hidden + ffn_share + vector_rows[5]
    output, second_pull = jax.vjp(layer_norm, resid_two, vector_rows[6], vector_rows[7])
    grad_two, grad_gain_two, grad_shift_two = second_pull(grad_out.astype(jnp.float32))
    grad_ffn_bias = jnp.sum(grad_two, axis=(0, 1))
    feedforward_gradient_total = lax.all_gather(
        grad_two.astype(jnp.bfloat16), "tensor", axis=1, tiled=True
    )
    grad_down = jnp.einsum(
        "ikn,ikb->nb",
        gelu_activations,
        feedforward_gradient_total,
        preferred_element_type=jnp.float32,
    )
    grad_activated = jnp.einsum(
        "rvq,nq->rvn",
        feedforward_gradient_total,
        down_weight_rows,
        preferred_element_type=jnp.float32,
    )
    gelu_value, gelu_pull = jax.vjp(gelu_exact, pre_act)
    grad_pre = gelu_pull(grad_activated)[0]
    grad_unit_bias = jnp.sum(grad_pre, axis=(0, 1))
    preactivation_gradient_reduced = grad_pre.astype(jnp.bfloat16)
    grad_up = jnp.einsum(
        "gqo,gqr->or",
        hidden_gathered,
        preactivation_gradient_reduced,
        preferred_element_type=jnp.float32,
    )
    hidden_part = jnp.einsum(
        "eon,in->eoi",
        preactivation_gradient_reduced,
        up_weight_columns,
        preferred_element_type=jnp.float32,
    )
    hidden_back = lax.psum_scatter(
        hidden_part.astype(jnp.bfloat16), "tensor", scatter_dimension=1, tiled=True
    ).astype(jnp.float32)
    norm_value, first_pull = jax.vjp(layer_norm, resid_one, vector_rows[3], vector_rows[4])
    grad_one, grad_gain_one, grad_shift_one = first_pull(grad_two + hidden_back)
    grad_attn_bias = jnp.sum(grad_one, axis=(0, 1))
    grad_one_low = grad_one.astype(jnp.bfloat16)
    first_norm_gradient_total = lax.all_gather(grad_one_low, "tensor", axis=1, tiled=True)
    grad_context = jnp.einsum(
        "yfb,qb->yfq",
        first_norm_gradient_total,
        output_weight_rows,
        preferred_element_type=jnp.float32,
    ).astype(jnp.bfloat16)
    grad_out_rows = jnp.einsum(
        "pwc,pwj->cj",
        attention_context,
        first_norm_gradient_total,
        preferred_element_type=jnp.float32,
    )
    grad_context = grad_context.reshape(head_shape)

    def backward_one(operands):
        return attend_backward(
            operands[0], operands[1], operands[2], operands[3], operands[4], operands[5]
        )

    grad_queries, grad_keys, grad_values = lax.map(
        backward_one, (queries, key_rows, values, lengths, log_sums, grad_context)
    )
    flat_shape = (seqs_here, seq_len, local_width)
    grad_queries = grad_queries.reshape(flat_shape)
    grad_keys = grad_keys.reshape(flat_shape)
    grad_values = grad_values.reshape(flat_shape)
    grad_query_bias = jnp.sum(grad_queries, axis=(0, 1))
    grad_value_bias = jnp.sum(grad_values, axis=(0, 1))
    projection_gradient = jnp.stack([grad_queries, grad_keys, grad_values]).astype(jnp.bfloat16)
    query_key_value_gradient = jnp.einsum(
        "waz,pway->pzy", token_gathered, projection_gradient, preferred_element_type=jnp.float32
    )
    input_part = jnp.einsum(
        "anqw,akw->nqk",
        projection_gradient,
        query_key_value_full,
        preferred_element_type=jnp.float32,
    )
    zeros_width = jnp.zeros((model_width,), jnp.float32)
    place_query = lax.dynamic_update_slice_in_dim(
        zeros_width, grad_query_bias, tensor_rank * local_width, 0
    )
    place_value = lax.dynamic_update_slice_in_dim(
        zeros_width, grad_value_bias, tensor_rank * local_width, 0
    )
    small_rows = jnp.stack(
        [
            place_query,
            place_value,
            grad_attn_bias,
            grad_gain_one,
            grad_shift_one,
            grad_ffn_bias,
            grad_gain_two,
            grad_shift_two,
        ]
    )
    unit_full = lax.dynamic_update_slice_in_dim(
        jnp.zeros((full_hidden,), jnp.float32), grad_unit_bias, tensor_rank * local_hidden, 0
    )
    small_copies = jnp.broadcast_to(small_rows[:, None, :], (8, tensor_count, model_width))
    unit_copies = jnp.broadcast_to(unit_full[None, None, :], (1, tensor_count, full_hidden))
    input_share, small_sum, unit_sum = (
        lax.psum_scatter(
            input_part.astype(jnp.bfloat16), "tensor", scatter_dimension=1, tiled=True
        ).astype(jnp.float32),
        lax.psum_scatter(
            small_copies.astype(jnp.bfloat16), "tensor", scatter_dimension=1, tiled=True
        ).astype(jnp.float32),
        lax.psum_scatter(
            unit_copies.astype(jnp.bfloat16), "tensor", scatter_dimension=1, tiled=True
        ).astype(jnp.float32),
    )
    grad_tokens = grad_one + input_share
    grad_qkv_out, grad_out_out, grad_up_out, grad_down_out, grad_vector_out, grad_bias_out = (
        lax.psum_scatter(query_key_value_gradient, "dp", scatter_dimension=1, tiled=True),
        lax.psum_scatter(grad_out_rows, "dp", scatter_dimension=1, tiled=True),
        lax.psum_scatter(grad_up, "dp", scatter_dimension=0, tiled=True),
        lax.psum_scatter(grad_down, "dp", scatter_dimension=1, tiled=True),
        lax.psum_scatter(small_sum[:, 0, :], "dp", scatter_dimension=1, tiled=True),
        lax.psum_scatter(unit_sum[0, 0], "dp", scatter_dimension=0, tiled=True),
    )
    return (
        output.astype(jnp.bfloat16),
        grad_tokens,
        grad_qkv_out,
        grad_out_out,
        grad_up_out,
        grad_down_out,
        grad_vector_out,
        grad_bias_out,
    )


def solution(mesh):
    in_specs = (
        P("dp", "tensor", None),
        P("dp"),
        P("dp", "tensor", None),
        P(None, "dp", "tensor"),
        P("tensor", "dp"),
        P("dp", "tensor"),
        P("tensor", "dp"),
        P(None, "dp"),
        P("dp"),
    )
    out_specs = (
        P("dp", "tensor", None),
        P("dp", "tensor", None),
        P(None, "dp", "tensor"),
        P("tensor", "dp"),
        P("dp", "tensor"),
        P("tensor", "dp"),
        P(None, "dp"),
        P("dp"),
    )
    return jax.shard_map(shards, mesh=mesh, in_specs=in_specs, out_specs=out_specs, check_vma=False)
```

profile of v0, /device:TPU:0, one launch (start us, length us, event | category | flops | bytes accessed | tf_op | source)
XLA Modules:
  0.0 879.0 jit_solution(11499733040699032781)
XLA Ops:
  8.8 28.1 %all-gather = bf16[8,96,8]{1,2,0:T(8,128)(2,1)S(1)} all-gather(bf16[1,96,8]{1,2,0:T(8,128)(2,1)} %bitcast.220), channel_id=1, replica_groups=mesh['dp'=8,'tensor'=4] {'dp'}, dimensions={0}, use_global_device_ids=true | all-gather | bytes 13824 | tf_op jit(solution)/shard_map/all_gather | solution.py:90
  39.8 31.4 %all_gather.33 = bf16[192,768]{0,1:T(8,128)(2,1)S(1)} all-gather(bf16[192,96]{0,1:T(8,128)(2,1)S(1)} %copy.45), channel_id=1, replica_groups=mesh['dp'=8,'tensor'=4] {'dp'}, dimensions={1}, use_global_device_ids=true | all-gather | bytes 331776 | tf_op jit(solution)/shard_map/all_gather | solution.py:87
  71.2 36.1 %all_gather.30 = bf16[3,768,192]{2,0,1:T(4,128)(2,1)S(1)} all-gather(bf16[3,96,192]{2,0,1:T(4,128)(2,1)S(1)} %copy.42), channel_id=1, replica_groups=mesh['dp'=8,'tensor'=4] {'dp'}, dimensions={1}, use_global_device_ids=true | all-gather | bytes 995328 | tf_op jit(solution)/shard_map/all_gather | solution.py:86
  107.3 5.2 fusion.59
  113.5 17.3 %while.26 = (s32[]{:T(128)}, bf16[4,512,3,64]{1,3,2,0:T(8,128)(2,1)S(1)}, f32[4,3,512,1]{2,1,3,0:T(4,128)}, bf16[4,512,3,64]{1,3,2,0:T(8,128)(2,1)S(1)}, s32[4]{...) while((s32[]{:T(128)}, ...), condition=%wide.region_3.4_spmd, body=%wide.region_0.3_spmd.sunk | while | flops 210861056 | bytes 10283621 | solution.py:118
  131.7 2.7 convolution_convert_fusion
  135.1 36.0 %reduce-scatter.18.cloned.1.call-done = bf16[4,128,768]{2,1,0:T(8,128)(2,1)} async-done(((bf16[4,512,768]{2,1,0:T(8,128)(2,1)}), bf16[4,128,768]{2,1,0:T(8,128)(2,1)}) %reduce-scatter.18.cloned.1.call-update) | async-done | bytes 786448 | tf_op jit(solution)/shard_map/reduce_scatter | solution.py:123
  174.3 2.0 fusion.75
  177.0 26.4 %all-gather.1 = bf16[8,1,384]{2,1,0:T(2,128)(2,1)S(1)} all-gather(bf16[1,1,384]{2,1,0:T(2,128)(2,1)S(1)} %reshape.168), channel_id=1, replica_groups=mesh['dp'=8,'tensor'=4] {'dp'}, dimensions={0}, use_global_device_ids=true | all-gather | bytes 6912 | tf_op jit(solution)/shard_map/all_gather | solution.py:91
  203.5 2.5 all-gather.11.cloned.1.call-done
  206.0 6.4 fusion.69
  212.5 2.6 copy-done.11
  215.1 15.5 %multiply_convert_fusion.1 = (bf16[4,512,768]{2,1,0:T(8,128)(2,1)}, f32[4,512,768]{2,1,0:T(8,128)}) fusion(f32[4,512,768]{2,1,0:T(8,128)S(1)} %get-tuple-element.200, f32[768]{0:T(1024)S(1)} %dynamic_slice.44, u8[512,768]{1,0:T(8,128)(4,1)S(1)} %get-tuple-element.130, u8[512,768]{1,0:T(8,128)(4,1)S(1)} %get-tuple-element.129), kind=kLoop, calls=%fused_computation.66 | loop fusion | flops 111673344 | bytes 16518144 | tf_op jit(solution)/shard_map/convert_element_type | solution.py:135
  230.6 18.9 %all-gather.15.cloned.1.call-done = bf16[768,768]{0,1:T(8,128)(2,1)} async-done(((bf16[768,96]{0,1:T(8,128)(2,1)}), bf16[768,768]{0,1:T(8,128)(2,1)}) %all-gather.15.cloned.1.call-update) | async-done | bytes 1179664 | tf_op jit(solution)/shard_map/all_gather | solution.py:89
  249.5 6.5 convolution_convert_fusion.2
  256.2 36.1 %reduce-scatter.20.cloned.1.call-done = bf16[4,128,768]{2,1,0:T(8,128)(2,1)} async-done(((bf16[4,512,768]{2,1,0:T(8,128)(2,1)}), bf16[4,128,768]{2,1,0:T(8,128)(2,1)}) %reduce-scatter.20.cloned.1.call-update) | async-done | bytes 786448 | tf_op jit(solution)/shard_map/reduce_scatter | solution.py:139
  292.3 2.0 fusion.93
  295.9 1.6 fusion.92
  299.7 28.1 %all-gather.17.cloned.1.call-done = bf16[4,512,768]{2,1,0:T(8,128)(2,1)} async-done(((bf16[4,128,768]{2,1,0:T(8,128)(2,1)}), bf16[4,512,768]{2,1,0:T(8,128)(2,1)}) %all-gather.17.cloned.1.call-update) | async-done | bytes 3145744 | tf_op jit(solution)/shard_map/all_gather | solution.py:146
  327.8 11.1 %fusion.98 = (bf16[768]{0:T(1024)(128)(2,1)}, bf16[4,512,768]{2,1,0:T(8,128)(2,1)S(1)}) fusion(f32[4,512,768]{2,1,0:T(8,128)} %get-tuple-element.184, bf16[4,512,768]{2,1,0:T(8,128)(2,1)} %all-gather.17.cloned.1.call-done, bf16[768,768]{0,1:T(8,128)(2,1)} %all-gather.15.cloned.1.call-done, f32[4,512,768]{2,1,0:T(8,128)} %copy-done.11, f32[768]{0:T(1024)} %copy-done.24), kind=kOutput, calls=%fused_computation.166 | convolution fusion | flops 2441084160 | bytes 20058624 | tf_op jit(solution)/shard_map/rvq,nq->rvn/dot_general | solution.py:155
  338.8 1.7 copy-done.39
  340.5 4.0 convolution_convert_fusion.1
  344.6 37.7 %reduce-scatter.22.cloned.1.call-done = bf16[4,128,768]{2,1,0:T(8,128)(2,1)} async-done(((bf16[4,512,768]{2,1,0:T(8,128)(2,1)}), bf16[4,128,768]{2,1,0:T(8,128)(2,1)}) %reduce-scatter.22.cloned.1.call-update) | async-done | bytes 786448 | tf_op jit(solution)/shard_map/reduce_scatter | solution.py:177
  382.3 2.8 multiply_reduce_fusion.1
  385.8 1.7 fusion.91
  390.4 28.1 %all-gather.19.cloned.1.call-done = bf16[4,512,768]{2,1,0:T(8,128)(2,1)} async-done(((bf16[4,128,768]{2,1,0:T(8,128)(2,1)}), bf16[4,512,768]{2,1,0:T(8,128)(2,1)}) %all-gather.19.cloned.1.call-update) | async-done | bytes 3145744 | tf_op jit(solution)/shard_map/all_gather | solution.py:184
  418.6 3.1 convolution_convert_fusion.3
  421.6 37.2 %while.27 = (s32[]{:T(128)}, f32[4,512,3,64]{1,3,2,0:T(8,128)}, bf16[4,512,3,64]{1,3,2,0:T(8,128)(2,1)}, f32[4,512,3,64]{1,3,2,0:T(8,128)}, bf16[4,512,3,64]{1,3...) while((s32[]{:T(128)}, f32[4,512,3,64]{1,3,2,0:T(8,128)}, ...), condition=%wide.region_17.18_spmd, body=%wide.region_15.17_spmd.sunk | while | flops 510589952 | bytes 32479416 | solution.py:204
  458.9 3.1 fusion.97
  462.1 3.0 fusion.96
  466.2 19.8 %reduce-scatter.30.cloned.1.call-done = bf16[8,1,768]{2,0,1:T(8,128)(2,1)} async-done(((bf16[8,4,768]{2,0,1:T(8,128)(2,1)}), bf16[8,1,768]{2,0,1:T(8,128)(2,1)}) %reduce-scatter.30.cloned.1.call-update) | async-done | bytes 12304 | tf_op jit(solution)/shard_map/reduce_scatter | solution.py:251
  487.7 3.4 convolution_bitcast_fusion.2
  491.1 5.8 fusion.70
  497.0 2.9 copy.67
  499.9 2.8 reshape.184
  502.8 6.5 bitcast_convert_fusion
  509.6 1.6 copy-done.13
  511.3 6.0 convolution_bitcast_fusion
  517.3 7.0 convolution_bitcast_fusion.1
  526.3 10.3 %all-reduce = bf16[1,4,3072]{2,1,0:T(4,128)(2,1)S(1)} all-reduce(bf16[1,4,3072]{2,1,0:T(4,128)(2,1)S(1)} %broadcast_in_dim.98), channel_id=12, replica_groups=mesh['dp'=8,'tensor'=4] {'tensor'}, use_global_device_ids=true, to_apply=%region_34.35.clone | all-reduce | flops 12288 | bytes 49152
  537.2 37.5 %all-reduce.1 = f32[3072]{0:T(1024)S(1)} all-reduce(f32[3072]{0:T(1024)S(1)} %bitcast.217), channel_id=13, replica_groups=mesh['dp'=8,'tensor'=4] {'dp'}, use_global_device_ids=true, to_apply=%region_35.36.clone | all-reduce | flops 3072 | bytes 24576
  576.8 38.7 %reduce-scatter.34.cloned.1.call-done = f32[96,192]{1,0:T(8,128)} async-done(((f32[768,192]{1,0:T(8,128)}), f32[96,192]{1,0:T(8,128)}) %reduce-scatter.34.cloned.1.call-update) | async-done | bytes 73744
  615.5 1.6 copy.70
  617.2 68.1 %reduce-scatter.32.cloned.1.call-done = f32[96,576]{1,0:T(8,128)} async-done(((f32[768,576]{1,0:T(8,128)}), f32[96,576]{1,0:T(8,128)}) %reduce-scatter.32.cloned.1.call-update) | async-done | bytes 221200
  687.2 37.2 %reduce-scatter.24.cloned.1.call-done = bf16[4,128,768]{2,1,0:T(8,128)(2,1)} async-done(((bf16[4,512,768]{2,1,0:T(8,128)(2,1)}), bf16[4,128,768]{2,1,0:T(8,128)(2,1)}) %reduce-scatter.24.cloned.1.call-update) | async-done | bytes 786448 | tf_op jit(solution)/shard_map/reduce_scatter | solution.py:248
  724.4 2.5 convert_add_fusion
  726.9 71.6 %reduce-scatter.28.cloned.1.call-done = f32[768,96]{0,1:T(8,128)} async-done(((f32[768,768]{0,1:T(8,128)}), f32[768,96]{0,1:T(8,128)}) %reduce-scatter.28.cloned.1.call-update) | async-done | bytes 294928 | tf_op jit(solution)/shard_map/reduce_scatter | solution.py:263
  798.5 73.0 %reduce-scatter.26.cloned.1.call-done = f32[96,768]{1,0:T(8,128)} async-done(((f32[768,768]{1,0:T(8,128)}), f32[96,768]{1,0:T(8,128)}) %reduce-scatter.26.cloned.1.call-update) | async-done | bytes 294928 | tf_op jit(solution)/shard_map/reduce_scatter | solution.py:262
  (246 shorter events, 80.9 us)
Async XLA Ops:
  8.0 99.3 %all-gather.9.cloned.1.call-start = ((), (), s32[]{:S(2)}) async-start(), calls=%async_computation.10 | async-start | bytes 3932160 | tf_op jit(solution)/shard_map/all_gather | solution.py:106
  8.7 162.4 %reduce-scatter.18.cloned.1.call-start = ((), (), s32[]{:S(2)}) async-start(), calls=%async_computation.11 | async-start | bytes 3932160 | tf_op jit(solution)/shard_map/reduce_scatter | solution.py:123
  107.3 5.2 copy-start.16
  130.8 3.7 copy-start.6
  130.8 3.7 copy-start.12
  130.8 3.7 copy-start.17
  131.7 39.5 %copy-start = (bf16[4,128,768]{2,1,0:T(8,128)(2,1)S(1)}, bf16[4,128,768]{2,1,0:T(8,128)(2,1)}, u32[]{:S(2)}) copy-start(bf16[4,128,768]{2,1,0:T(8,128)(2,1)} %param.13) | copy-start | bytes 2359300
  134.5 69.0 %all-gather.13.cloned.1.call-start = ((), (), s32[]{:S(2)}) async-start(), calls=%async_computation.13 | async-start | bytes 1327104 | tf_op jit(solution)/shard_map/all_gather | solution.py:88
  135.1 70.9 %all-gather.11.cloned.1.call-start = ((), (), s32[]{:S(2)}) async-start(), calls=%async_computation.12 | async-start | bytes 3932160 | tf_op jit(solution)/shard_map/all_gather | solution.py:128
  171.2 3.2 copy-start.1
  171.2 5.9 copy-start.31
  174.3 2.7 copy-start.22
  176.4 73.2 %all-gather.15.cloned.1.call-start = ((), (), s32[]{:S(2)}) async-start(), calls=%async_computation.14 | async-start | bytes 1327104 | tf_op jit(solution)/shard_map/all_gather | solution.py:89
  177.0 115.3 %reduce-scatter.20.cloned.1.call-start = ((), (), s32[]{:S(2)}) async-start(), calls=%async_computation.15 | async-start | bytes 3932160 | tf_op jit(solution)/shard_map/reduce_scatter | solution.py:139
  203.5 8.9 %copy-start.24 = (f32[768]{0:T(1024)}, f32[768]{0:T(1024)S(1)}, u32[]{:S(2)}) copy-start(f32[768]{0:T(1024)S(1)} %dynamic_slice.44) | copy-start | bytes 9220
  212.5 2.7 copy-start.11
  256.1 36.2 %copy-start.20 = (f32[768]{0:T(1024)S(1)}, f32[768]{0:T(1024)}, u32[]{:S(2)}) copy-start(f32[768]{0:T(1024)} %get-tuple-element.140) | copy-start | bytes 9220
  256.1 36.2 %copy-start.25 = (f32[768]{0:T(1024)S(1)}, f32[768]{0:T(1024)}, u32[]{:S(2)}) copy-start(f32[768]{0:T(1024)} %get-tuple-element.139) | copy-start | bytes 9220
  256.1 38.5 %copy-start.8 = (bf16[4,128,768]{2,1,0:T(8,128)(2,1)S(1)}, bf16[4,128,768]{2,1,0:T(8,128)(2,1)}, u32[]{:S(2)}) copy-start(bf16[4,128,768]{2,1,0:T(8,128)(2,1)} %param.15) | copy-start | bytes 2359300
  256.1 38.5 %copy-start.18 = (f32[768]{0:T(1024)S(1)}, f32[768]{0:T(1024)}, u32[]{:S(2)}) copy-start(f32[768]{0:T(1024)} %get-tuple-element.137) | copy-start | bytes 9220
  256.1 71.6 %all-gather.17.cloned.1.call-start = ((), (), s32[]{:S(2)}) async-start(), calls=%async_computation.16 | async-start | bytes 3932160 | tf_op jit(solution)/shard_map/all_gather | solution.py:146
  292.2 3.6 copy-start.9
  292.2 3.6 copy-start.19
  292.2 3.6 copy-start.23
  299.1 83.2 %reduce-scatter.22.cloned.1.call-start = ((), (), s32[]{:S(2)}) async-start(), calls=%async_computation.17 | async-start | bytes 3932160 | tf_op jit(solution)/shard_map/reduce_scatter | solution.py:177
  327.8 12.7 %copy-start.32 = (bf16[768,768]{1,0:T(8,128)(2,1)S(1)}, bf16[768,768]{1,0:T(8,128)(2,1)}, u32[]{:S(2)}) copy-start(bf16[768,768]{1,0:T(8,128)(2,1)} %all-gather.13.cloned.1.call-done) | copy-start | bytes 3538948
  344.5 74.0 %all-gather.19.cloned.1.call-start = ((), (), s32[]{:S(2)}) async-start(), calls=%async_computation.18 | async-start | bytes 3932160 | tf_op jit(solution)/shard_map/all_gather | solution.py:184
  382.3 3.5 copy-start.14
  387.5 2.6 copy-start.10
  387.5 2.8 copy-start.26
  387.5 2.8 copy-start.29
  387.6 2.8 copy-start.28
  387.6 2.8 copy-start.27
  389.9 31.8 %copy-start.5 = (bf16[4,512,3,64]{1,3,2,0:T(8,128)(2,1)S(1)}, bf16[4,512,3,64]{1,3,2,0:T(8,128)(2,1)}, u32[]{:S(2)}) copy-start(bf16[4,512,3,64]{1,3,2,0:T(8,128)(2,1)} %copy-done.4) | copy-start | bytes 2359300
  389.9 31.8 %copy-start.7 = (bf16[4,512,3,64]{1,3,2,0:T(8,128)(2,1)S(1)}, bf16[4,512,3,64]{1,3,2,0:T(8,128)(2,1)}, u32[]{:S(2)}) copy-start(bf16[4,512,3,64]{1,3,2,0:T(8,128)(2,1)} %copy-done.6) | copy-start | bytes 2359300
  389.9 31.8 %copy-start.36 = (s32[4]{0:T(128)S(1)}, s32[4]{0:T(128)}, u32[]{:S(2)}) copy-start(s32[4]{0:T(128)} %param.14) | copy-start | bytes 52
  389.9 96.0 %reduce-scatter.30.cloned.1.call-start = ((), (), s32[]{:S(2)}) async-start(), calls=%async_computation.22 | async-start | bytes 61440 | tf_op jit(solution)/shard_map/reduce_scatter | solution.py:251
  458.8 28.8 %copy-start.15 = (bf16[4,512,768]{2,1,0:T(8,128)(2,1)S(1)}, bf16[4,512,768]{2,1,0:T(8,128)(2,1)}, u32[]{:S(2)}) copy-start(bf16[4,512,768]{2,1,0:T(8,128)(2,1)} %all-gather.19.cloned.1.call-done) | copy-start | bytes 9437188
  466.1 109.2 %reduce-scatter.36.cloned.1.call-start = ((), (), s32[]{:S(2)}) async-start(), calls=%async_computation.25 | async-start | bytes 442368
  487.6 127.9 %reduce-scatter.34.cloned.1.call-start = ((), (), s32[]{:S(2)}) async-start(), calls=%async_computation.24 | async-start | bytes 884736
  491.1 194.2 %reduce-scatter.32.cloned.1.call-start = ((), (), s32[]{:S(2)}) async-start(), calls=%async_computation.23 | async-start | bytes 2211840
  502.8 221.6 %reduce-scatter.24.cloned.1.call-start = ((), (), s32[]{:S(2)}) async-start(), calls=%async_computation.19 | async-start | bytes 3932160 | tf_op jit(solution)/shard_map/reduce_scatter | solution.py:248
  509.4 289.1 %reduce-scatter.28.cloned.1.call-start = ((), (), s32[]{:S(2)}) async-start(), calls=%async_computation.21 | async-start | bytes 2654208 | tf_op jit(solution)/shard_map/reduce_scatter | solution.py:263
  517.2 7.1 copy-start.38
  517.3 7.7 copy-start.37
  517.3 8.9 %copy-start.30 = (bf16[768]{0:T(1024)(128)(2,1)S(1)}, bf16[768]{0:T(1024)(128)(2,1)}, u32[]{:S(2)}) copy-start(bf16[768]{0:T(1024)(128)(2,1)} %get-tuple-element.201) | copy-start | bytes 4612
  517.3 354.2 %reduce-scatter.26.cloned.1.call-start = ((), (), s32[]{:S(2)}) async-start(), calls=%async_computation.20 | async-start | bytes 2654208 | tf_op jit(solution)/shard_map/reduce_scatter | solution.py:262
  524.3 200.1 %copy-start.3 = (f32[4,128,768]{2,1,0:T(8,128)S(1)}, f32[4,128,768]{2,1,0:T(8,128)}, u32[]{:S(2)}) copy-start(f32[4,128,768]{2,1,0:T(8,128)} %copy-done.2) | copy-start | bytes 4718596
  (14 other events, 18.6 us)
Sparse Core Ops, SparseCore 0:
  10.4 31.2 all-gather.8
  134.6 36.5 reduce-scatter.17
  299.2 28.4 all-gather.16
  390.0 28.4 all-gather.18
  466.2 19.6 reduce-scatter.29
Sparse Core Ops, SparseCore 1:
  137.2 40.0 all-gather.12
  179.3 26.7 all-gather.10
  208.1 41.4 all-gather.14
  256.2 36.0 reduce-scatter.19
  344.6 37.6 reduce-scatter.21
  487.7 62.3 reduce-scatter.35
  553.2 62.3 reduce-scatter.33
  618.9 66.3 reduce-scatter.31
  687.7 36.6 reduce-scatter.23
  728.5 69.9 reduce-scatter.27
  802.4 69.0 reduce-scatter.25
where the time goes:
time: 887 us; the launch traced here: 879 us
  waiting for transfers between devices  498 us (56%)
  blocking collectives  170 us (19%)
  matrix products  97.1 us (11%)
  other arithmetic  57.4 us (6%)
  local copies, waits for them, and re-layouts  38.1 us (4%)
  between operations  17.1 us (2%)
    unnamed x19, waiting for transfers between devices  109 us
    reduce_scatter x1, waiting for transfers between devices, shards(): lax.psum_scatter(grad_up, 'dp', scatter_dimension=0, tiled=True)  73 us
    reduce_scatter x1, waiting for transfers between devices, shards(): lax.psum_scatter(grad_down, 'dp', scatter_dimension=1, tiled=True)  71.6 us
    unnamed x2, blocking collectives  47.7 us
    reduce_scatter x1, waiting for transfers between devices, shards(): lax.psum_scatter(hidden_part.astype(jnp.bfloat16), 'tensor', scatter_dime...  37.7 us
    reduce_scatter x1, waiting for transfers between devices, shards(): lax.psum_scatter(input_part.astype(jnp.bfloat16), 'tensor', scatter_dimen...  37.2 us
    all_gather x1, blocking collectives, shards(): lax.all_gather(qkv_weight, 'dp', axis=1, tiled=True)  36.1 us
    reduce_scatter x1, waiting for transfers between devices, shards(): lax.psum_scatter(feedforward_portion.astype(jnp.bfloat16), 'tensor', scat...  36.1 us
  transfers between devices with their start and end apart: 16, of which 13 were waited for; matrix products, arithmetic and copies ran while one was open for 9% of the time, Pallas kernels for 0%

commit v1 on v0

v1 whole, which is shorter than its diff:
```python
import functools

import jax
import jax.numpy as jnp
import numpy as np
from jax import lax
from jax.experimental import pallas as pl
from jax.experimental.pallas import tpu as pltpu
from jax.sharding import PartitionSpec as P

HD = 64
EPS = 1e-12
NEG = -1e30
F32 = jnp.float32
BF16 = jnp.bfloat16
VMEM_LIMIT = 67043328
ROWS = 128


def dot(left, right):
    return lax.dot_general(left, right, (((1,), (0,)), ((), ())), preferred_element_type=F32)


def dot_nt(left, right):
    return lax.dot_general(left, right, (((1,), (1,)), ((), ())), preferred_element_type=F32)


def lane_masks(scale):
    lane = lax.broadcasted_iota(jnp.int32, (1, 128), 1)
    low = jnp.where(lane < HD, F32(scale), F32(0)).astype(BF16)
    high = jnp.where(lane < HD, F32(0), F32(scale)).astype(BF16)
    return low, high


def is_low(shape):
    return lax.broadcasted_iota(jnp.int32, shape, 1) < HD


def put_row(ref, row, span, value):
    old = ref[8:16, span]
    here = lax.broadcasted_iota(jnp.int32, old.shape, 0) == row
    ref[8:16, span] = jnp.where(here, value, old)


def forward_kernel(
    x_ref, go_ref, len_ref, w_ref, sm_ref,
    out_ref, qkv_ref, ctx_ref, act_ref, gp_ref, hb_ref, n1_ref, s1_ref, g2_ref, stat_ref, gsm_ref,
    acc, hid, pre,
):
    seq, width = x_ref.shape
    blocks = seq // ROWS
    low, high = lane_masks(0.125)
    length = len_ref[0, 0]
    key_bias = jnp.where(lax.broadcasted_iota(jnp.int32, (1, seq), 1) < length, F32(0), F32(NEG))

    acc[...] = jnp.zeros_like(acc)

    @pl.loop(0, 4)
    def _(t):
        proj = dot(x_ref[...], w_ref[0, t, :, 0:640]) + sm_ref[pl.ds(12 + t, 1), 0:640]
        qkv_ref[t, :, 0:640] = proj.astype(BF16)
        q_two = pltpu.roll(jnp.where(is_low((seq, 128)), proj[:, 384:512] * 0.125, 0.0), 64, 1)
        qkv_ref[t, :, 640:768] = q_two.astype(BF16)

        @pl.loop(0, seq // 256)
        def _(r):
            rows = pl.ds(pl.multiple_of(r * 256, 256), 256)
            q_pair = qkv_ref[t, rows, 0:128]
            outs = []
            stats = []
            for h in range(3):
                if h < 2:
                    queries = q_pair * (low, high)[h]
                    keys = qkv_ref[t, :, 128:256]
                    values = qkv_ref[t, :, 256:384]
                else:
                    queries = qkv_ref[t, rows, 640:768]
                    keys = qkv_ref[t, :, 384:512]
                    values = qkv_ref[t, :, 512:640]
                scores = dot_nt(queries, keys) + key_bias
                highest = jnp.max(scores, axis=1, keepdims=True)
                grown = jnp.exp(scores - highest)
                total = jnp.sum(grown, axis=1, keepdims=True)
                probs = (grown * (1.0 / total)).astype(BF16)
                outs.append(dot(probs, values))
                stats.append(highest + jnp.log(total))
            lowest = is_low((256, 128))
            ctx_ref[t, rows, 0:128] = jnp.where(lowest, pltpu.roll(outs[2], 64, 1), 0.0).astype(BF16)
            ctx_ref[t, rows, 128:256] = jnp.where(lowest, outs[0], outs[1]).astype(BF16)
            lane = lax.broadcasted_iota(jnp.int32, (256, 128), 1)
            stat = jnp.where(lane == 0, stats[0], jnp.where(lane == 1, stats[1], stats[2]))
            stat_ref[t, rows, :] = stat

        acc[...] += dot_nt(ctx_ref[t], w_ref[0, t, :, 512:768])

    @pl.loop(0, blocks)
    def _(r):
        rows = pl.ds(pl.multiple_of(r * ROWS, ROWS), ROWS)
        resid = x_ref[rows, :].astype(F32) + acc[rows, :] + sm_ref[2:3, :]
        centred = resid - jnp.mean(resid, axis=1, keepdims=True)
        scale = lax.rsqrt(jnp.mean(centred * centred, axis=1, keepdims=True) + EPS)
        normed = centred * scale
        hidden = normed * sm_ref[3:4, :] + sm_ref[4:5, :]
        n1_ref[rows, :] = normed
        s1_ref[rows, :] = jnp.broadcast_to(scale, (ROWS, 128))
        hid[rows, :] = hidden
        hb_ref[rows, :] = hidden.astype(BF16)
        acc[rows, :] = hidden + sm_ref[5:6, :]

    @pl.loop(0, 4)
    def _(t):
        pre[...] = dot(hb_ref[...], w_ref[1, t])

        @pl.loop(0, blocks)
        def _(r):
            rows = pl.ds(pl.multiple_of(r * ROWS, ROWS), ROWS)
            u = pre[rows, :] + sm_ref[pl.ds(8 + t, 1), :]
            cdf = 0.5 + 0.5 * lax.erf(u * F32(np.sqrt(0.5)))
            density = jnp.exp(u * u * -0.5) * F32(1.0 / np.sqrt(2.0 * np.pi))
            act_ref[t, rows, :] = (u * cdf).astype(BF16)
            gp_ref[t, rows, :] = cdf + u * density

        acc[...] += dot_nt(act_ref[t], w_ref[2, t])

    gsm_ref[...] = jnp.zeros_like(gsm_ref)

    @pl.loop(0, blocks)
    def _(r):
        rows = pl.ds(pl.multiple_of(r * ROWS, ROWS), ROWS)
        resid = acc[rows, :]
        centred = resid - jnp.mean(resid, axis=1, keepdims=True)
        scale = lax.rsqrt(jnp.mean(centred * centred, axis=1, keepdims=True) + EPS)
        normed = centred * scale
        gain = sm_ref[6:7, :]
        out_ref[rows, :] = (normed * gain + sm_ref[7:8, :]).astype(BF16)
        cot = go_ref[rows, :].astype(F32)
        e = cot * gain
        en = jnp.mean(e * normed, axis=1, keepdims=True)
        grad = scale * (e - jnp.mean(e, axis=1, keepdims=True) - normed * en)
        g2_ref[rows, :] = grad
        gsm_ref[5:6, :] += jnp.sum(grad, axis=0, keepdims=True)
        gsm_ref[6:7, :] += jnp.sum(cot * normed, axis=0, keepdims=True)
        gsm_ref[7:8, :] += jnp.sum(cot, axis=0, keepdims=True)


def backward_kernel(
    x_ref, len_ref, w_ref, sm_ref, qkv_ref, ctx_ref, act_ref, gp_ref, hb_ref, n1_ref, s1_ref, g2_ref, stat_ref,
    gsm_in,
    gtok_ref, g_ref, gsm_ref,
    acc, low_grad, tall, gpre, gctx, gpacked,
):
    seq, width = x_ref.shape
    blocks = seq // ROWS
    low, high = lane_masks(0.125)
    one_low, one_high = lane_masks(1.0)
    length = len_ref[0, 0]
    key_bias = jnp.where(lax.broadcasted_iota(jnp.int32, (seq, 1), 0) < length, F32(0), F32(NEG))
    gsm_ref[0:8, :] = gsm_in[0:8, :]
    gsm_ref[8:16, :] = jnp.zeros((8, gsm_ref.shape[1]), F32)

    low_grad[...] = g2_ref[...].astype(BF16)
    tall[0] = jnp.transpose(g2_ref[...]).astype(BF16)
    tall[1] = jnp.transpose(hb_ref[...].astype(F32)).astype(BF16)
    acc[...] = g2_ref[...]

    @pl.loop(0, 4)
    def _(t):
        g_ref[2, t] = dot(tall[0], act_ref[t]).astype(BF16)
        grad_act = dot(low_grad[...], w_ref[2, t])
        grad_pre = grad_act * gp_ref[t]
        put_row(gsm_ref, t, slice(0, 768), jnp.sum(grad_pre, axis=0, keepdims=True))
        gpre[...] = grad_pre.astype(BF16)
        g_ref[1, t] = dot(tall[1], gpre[...]).astype(BF16)
        acc[...] += dot_nt(gpre[...], w_ref[1, t])

    @pl.loop(0, blocks)
    def _(r):
        rows = pl.ds(pl.multiple_of(r * ROWS, ROWS), ROWS)
        cot = acc[rows, :]
        normed = n1_ref[rows, :]
        e = cot * sm_ref[3:4, :]
        en = jnp.mean(e * normed, axis=1, keepdims=True)
        grad = s1_ref[rows, 0:1] * (e - jnp.mean(e, axis=1, keepdims=True) - normed * en)
        acc[rows, :] = grad
        low_grad[rows, :] = grad.astype(BF16)
        gsm_ref[2:3, :] += jnp.sum(grad, axis=0, keepdims=True)
        gsm_ref[3:4, :] += jnp.sum(cot * normed, axis=0, keepdims=True)
        gsm_ref[4:5, :] += jnp.sum(cot, axis=0, keepdims=True)

    tall[0] = jnp.transpose(acc[...]).astype(BF16)
    tall[1] = jnp.transpose(x_ref[...].astype(F32)).astype(BF16)

    @pl.loop(0, 4)
    def _(t):
        back = dot(low_grad[...], w_ref[0, t, :, 512:768])
        gctx[:, 0:128] = pltpu.roll(jnp.where(is_low((seq, 128)), back[:, 0:128], 0.0), 64, 1).astype(BF16)
        gctx[:, 128:256] = back[:, 128:256].astype(BF16)
        log_rows = jnp.transpose(stat_ref[t])
        grads_q = []
        grads_k = []
        grads_v = []
        for h in range(3):
            if h < 2:
                queries = qkv_ref[t, :, 0:128] * (low, high)[h]
                keys = qkv_ref[t, :, 128:256]
                values = qkv_ref[t, :, 256:384]
                cots = gctx[:, 128:256] * (one_low, one_high)[h]
            else:
                queries = qkv_ref[t, :, 640:768]
                keys = qkv_ref[t, :, 384:512]
                values = qkv_ref[t, :, 512:640]
                cots = gctx[:, 0:128]
            scores = dot_nt(keys, queries) + key_bias
            probs = jnp.exp(scores - log_rows[h : h + 1, :])
            grad_probs = dot_nt(values, cots)
            row_dots = jnp.sum(grad_probs * probs, axis=0, keepdims=True)
            grad_scores = (probs * (grad_probs - row_dots)).astype(BF16)
            grads_v.append(dot(probs.astype(BF16), cots))
            grads_k.append(dot(grad_scores, queries))
            part = (0, HD, HD)[h]
            keys_tall = jnp.transpose(keys.astype(F32))[part : part + HD, :].astype(BF16)
            grads_q.append(dot(keys_tall, grad_scores) * 0.125)
        pair = jnp.transpose(jnp.concatenate([grads_q[0], grads_q[1]], axis=0))
        single = jnp.transpose(jnp.concatenate([grads_q[2], jnp.zeros_like(grads_q[2])], axis=0))
        tiles = [pair, grads_k[0] + grads_k[1], grads_v[0] + grads_v[1], single + grads_k[2], grads_v[2]]
        for i, tile in enumerate(tiles):
            span = slice(128 * i, 128 * i + 128)
            put_row(gsm_ref, 4 + t, span, jnp.sum(tile, axis=0, keepdims=True))
            gpacked[:, span] = tile.astype(BF16)
        g_ref[0, t, :, 0:512] = dot(tall[1], gpacked[:, 0:512]).astype(BF16)
        g_ref[0, t, :, 512:640] = (
            dot(tall[1], gpacked[:, 512:640]) + dot(tall[0], ctx_ref[t, :, 0:128])
        ).astype(BF16)
        g_ref[0, t, :, 640:768] = dot(tall[0], ctx_ref[t, :, 128:256]).astype(BF16)
        acc[...] += dot_nt(gpacked[...], w_ref[0, t, :, 0:640])

    gtok_ref[...] = acc[...].astype(BF16)


def forward_call(x, go, length, w, sm):
    seq, width = x.shape
    shapes = (
        ((seq, width), BF16), ((4, seq, 768), BF16), ((4, seq, 256), BF16), ((4, seq, 768), BF16),
        ((4, seq, 768), F32), ((seq, width), BF16), ((seq, width), F32), ((seq, 128), F32),
        ((seq, width), F32), ((4, seq, 128), F32), ((16, width), F32),
    )
    vmem = pl.BlockSpec(memory_space=pltpu.VMEM)
    smem = pl.BlockSpec(memory_space=pltpu.SMEM)
    return pl.pallas_call(
        forward_kernel,
        out_shape=[jax.ShapeDtypeStruct(s, d) for s, d in shapes],
        in_specs=[vmem, vmem, smem, vmem, vmem],
        out_specs=[vmem] * len(shapes),
        scratch_shapes=[pltpu.VMEM((seq, width), F32)] * 3,
        compiler_params=pltpu.CompilerParams(vmem_limit_bytes=VMEM_LIMIT),
        name="forward",
    )(x, go, length, w, sm)


def backward_call(x, length, w, sm, saved, gsm):
    seq, width = x.shape
    shapes = (((seq, width), BF16), ((3, 4, width, 768), BF16), ((16, width), F32))
    vmem = pl.BlockSpec(memory_space=pltpu.VMEM)
    smem = pl.BlockSpec(memory_space=pltpu.SMEM)
    return pl.pallas_call(
        backward_kernel,
        out_shape=[jax.ShapeDtypeStruct(s, d) for s, d in shapes],
        in_specs=[vmem, smem] + [vmem] * (3 + len(saved)),
        out_specs=[vmem] * len(shapes),
        scratch_shapes=[
            pltpu.VMEM((seq, width), F32), pltpu.VMEM((seq, width), BF16), pltpu.VMEM((2, width, seq), BF16),
            pltpu.VMEM((seq, 768), BF16), pltpu.VMEM((seq, 256), BF16), pltpu.VMEM((seq, 640), BF16),
        ],
        compiler_params=pltpu.CompilerParams(vmem_limit_bytes=VMEM_LIMIT),
        name="backward",
    )(x, length, w, sm, *saved, gsm)


def pack_attention(q, k, v, o):
    return jnp.concatenate(
        [q[:, :128], k[:, :128], v[:, :128], q[:, 128:], k[:, 128:], o[:, 128:], v[:, 128:], o[:, :128]], axis=1
    )


def shards(tokens, lengths, grad_out, qkv_weight, out_weight, up_weight, down_weight, vectors, hidden_bias):
    dp_count = lax.axis_size("dp")
    tensor_count = lax.axis_size("tensor")
    dp_rank = lax.axis_index("dp")
    tensor_rank = lax.axis_index("tensor")
    width = tokens.shape[2]
    seq = tokens.shape[1] * tensor_count
    part = width // dp_count

    own = jnp.stack([
        pack_attention(qkv_weight[0], qkv_weight[1], qkv_weight[2], out_weight.T), up_weight, down_weight.T
    ])
    w = lax.all_gather(lax.all_gather(own, "dp", axis=1, tiled=True), "tensor", axis=1)
    vec = lax.all_gather(vectors, "dp", axis=1, tiled=True).astype(F32)
    hb = lax.all_gather(hidden_bias, "dp", axis=0, tiled=True).astype(F32).reshape(4, 768)
    qb = vec[0].reshape(4, 192)
    vb = vec[1].reshape(4, 192)
    none = jnp.zeros((4, 128), F32)
    qkvb = jnp.concatenate(
        [qb[:, :128], none, vb[:, :128], qb[:, 128:], none, vb[:, 128:], none], axis=1
    )
    sm = jnp.concatenate([vec, hb, qkvb], axis=0)
    x = lax.all_to_all(tokens, "tensor", 0, 1, tiled=True)[0]
    go = lax.all_to_all(grad_out, "tensor", 0, 1, tiled=True)[0]
    length = lax.dynamic_slice_in_dim(lengths, tensor_rank, 1).reshape(1, 1)

    out, *saved, gsm = forward_call(x, go, length, w, sm)
    gtok, grads, gsm = backward_call(x, length, w, sm, saved, gsm)

    output = lax.all_to_all(out[None], "tensor", 1, 0, tiled=True)
    grad_tokens = lax.all_to_all(gtok[None], "tensor", 1, 0, tiled=True).astype(F32)
    g = lax.psum_scatter(grads, "tensor", scatter_dimension=1)
    g = lax.psum_scatter(g, "dp", scatter_dimension=1, tiled=True).astype(F32)
    a = g[0]
    gq = jnp.concatenate([a[:, 0:128], a[:, 384:448]], axis=1)
    gk = jnp.concatenate([a[:, 128:256], a[:, 448:512]], axis=1)
    gv = jnp.concatenate([a[:, 256:384], a[:, 576:640]], axis=1)
    gout = jnp.concatenate([a[:, 640:768], a[:, 512:576]], axis=1).T
    gsm = lax.psum(gsm, ("dp", "tensor"))
    packed = gsm[12:16]
    row_q = jnp.concatenate([packed[:, 0:128], packed[:, 384:448]], axis=1).reshape(1, width)
    row_v = jnp.concatenate([packed[:, 256:384], packed[:, 576:640]], axis=1).reshape(1, width)
    rows = jnp.concatenate([row_q, row_v, gsm[2:8]], axis=0)
    grad_vectors = lax.dynamic_slice_in_dim(rows, dp_rank * part, part, 1)
    units = gsm[8:12].reshape(-1)
    grad_bias = lax.dynamic_slice_in_dim(units, dp_rank * (part * 4), part * 4)
    return output, grad_tokens, jnp.stack([gq, gk, gv]), gout, g[1], g[2].T, grad_vectors, grad_bias


def solution(mesh):
    in_specs = (
        P("dp", "tensor", None), P("dp"), P("dp", "tensor", None), P(None, "dp", "tensor"), P("tensor", "dp"),
        P("dp", "tensor"), P("tensor", "dp"), P(None, "dp"), P("dp"),
    )
    out_specs = (
        P("dp", "tensor", None), P("dp", "tensor", None), P(None, "dp", "tensor"), P("tensor", "dp"),
        P("dp", "tensor"), P("tensor", "dp"), P(None, "dp"), P("dp"),
    )
    return jax.shard_map(shards, mesh=mesh, in_specs=in_specs, out_specs=out_specs, check_vma=False)
```

time: 887 us -> 615 us (0.69)
  waiting for transfers between devices: 498 us -> 346 us
  matrix products: 97.1 us -> 0 us
  Pallas kernels: 0 us -> 90.9 us
  blocking collectives: 170 us -> 115 us
  other arithmetic: 57.4 us -> 15.8 us
  local copies, waits for them, and re-layouts: 38.1 us -> 20.9 us
  starting transfers between devices: 1.59 us -> 11.6 us
    reduce_scatter x7 -> x1, waiting for transfers between devices: 311 us -> 0.01 us  [shards(): g = lax.psum_scatter(g, 'dp', scatter_dimension=1, tiled=True).astype(F32)]
    unnamed x19 -> x5, waiting for transfers between devices: 109 us -> 244 us
    dot_general x40 -> x0, matrix products: 97.1 us -> none  [the longest x1 11.1 us: shards(): jnp.einsum('rvq,nq->rvn', feedforward_gradient_total, down_weight_rows, p...]
    pallas_call x0 -> x2, Pallas kernels: none -> 90.9 us  [the longest x1 47.6 us: backward_call(): pl.pallas_call(backward_kernel, out_shape=[jax.ShapeDtypeStruct(s, d) for...]
    all_gather x4 -> x2, blocking collectives: 122 us -> 52.1 us  [the longest x1 26.1 us: shards(): vec = lax.all_gather(vectors, 'dp', axis=1, tiled=True).astype(F32)]
    unnamed x2 -> x0, blocking collectives: 47.7 us -> none
    psum x0 -> x1, blocking collectives: none -> 46.3 us  [shards(): gsm = lax.psum(gsm, ('dp', 'tensor'))]
    reduce_sum x16 -> x0, other arithmetic: 22.9 us -> none  [the longest x3 4.26 us: layer_norm(): return centred * lax.rsqrt(spread + 1e-12) * norm_gain + norm_shift]
  transfers between devices with their start and end apart: 16 -> 7, of which waited for: 13 -> 4; matrix products, arithmetic and copies ran while one was open for 9% -> 4% of each run, Pallas kernels for 0% -> 0%
where the time goes in v1:
time: 615 us; the launch traced here: 614 us
  waiting for transfers between devices  346 us (56%)
  blocking collectives  115 us (19%)
  Pallas kernels  90.9 us (15%)
  local copies, waits for them, and re-layouts  20.9 us (3%)
  other arithmetic  15.8 us (3%)
  between operations  14.1 us (2%)
  starting transfers between devices  11.6 us (2%)
    unnamed x5, waiting for transfers between devices  244 us
    all_gather x1, waiting for transfers between devices, shards(): lax.all_gather(own, 'dp', axis=1, tiled=True)  67.4 us
    pallas_call x1, Pallas kernels, backward_call(): pl.pallas_call(backward_kernel, out_shape=[jax.ShapeDtypeStruct(s, d) for...  47.6 us
    psum x1, blocking collectives, shards(): gsm = lax.psum(gsm, ('dp', 'tensor'))  46.3 us
    pallas_call x1, Pallas kernels, forward_call(): pl.pallas_call(forward_kernel, out_shape=[jax.ShapeDtypeStruct(s, d) for...  43.3 us
    all_gather x1, waiting for transfers between devices, shards(): lax.all_gather(lax.all_gather(own, 'dp', axis=1, tiled=True), 'tensor', a...  26.4 us
    all_gather x1, blocking collectives, shards(): vec = lax.all_gather(vectors, 'dp', axis=1, tiled=True).astype(F32)  26.1 us
    all_gather x1, blocking collectives, shards(): lax.all_gather(hidden_bias, 'dp', axis=0, tiled=True).astype(F32)  26 us
  transfers between devices with their start and end apart: 7, of which 4 were waited for; matrix products, arithmetic and copies ran while one was open for 4% of the time, Pallas kernels for 0%

profile of v1, /device:TPU:0, one launch (start us, length us, event | category | flops | bytes accessed | tf_op | source)
XLA Modules:
  0.0 614.0 jit_solution(9149218509302155426)
XLA Ops:
  7.2 0.9 slice_bitcast_fusion.3
  8.2 0.9 copy.25
  9.1 0.1 concatenate.30
  9.2 1.8 pad_maximum_fusion
  11.1 67.4 %all-gather.6.cloned.1.call-done = bf16[3,768,768]{2,1,0:T(8,128)(2,1)} async-done(((bf16[3,96,768]{2,1,0:T(8,128)(2,1)}), bf16[3,768,768]{2,1,0:T(8,128)(2,1)}) %all-gather.6.cloned.1.call-update) | async-done | bytes 3538960 | tf_op jit(solution)/shard_map/all_gather | solution.py:297
  78.6 16.5 %all_to_all.19 = bf16[4,128,768]{2,1,0:T(8,128)(2,1)} all-to-all(bf16[4,128,768]{2,1,0:T(8,128)(2,1)S(1)} %copy-done), channel_id=1, replica_groups=mesh['dp'=8,'tensor'=4] {'tensor'}, dimensions={0} | all-to-all | bytes 1572864 | tf_op jit(solution)/shard_map/all_to_all | solution.py:307
  95.1 4.2 all-to-all-start.1
  99.3 26.1 %all-gather.1 = bf16[8,96,8]{1,2,0:T(8,128)(2,1)S(1)} all-gather(bf16[1,96,8]{1,2,0:T(8,128)(2,1)S(1)} %bitcast.78), channel_id=1, replica_groups=mesh['dp'=8,'tensor'=4] {'dp'}, dimensions={0}, use_global_device_ids=true | all-gather | bytes 13824 | tf_op jit(solution)/shard_map/all_gather | solution.py:298
  125.5 0.1 reshape.67
  125.6 0.1 reshape_squeeze.6
  125.7 0.1 reshape_squeeze.7
  125.8 26.0 %all-gather.2 = bf16[8,1,384]{2,1,0:T(2,128)(2,1)S(1)} all-gather(bf16[1,1,384]{2,1,0:T(2,128)(2,1)S(1)} %reshape.62), channel_id=1, replica_groups=mesh['dp'=8,'tensor'=4] {'dp'}, dimensions={0}, use_global_device_ids=true | all-gather | bytes 6912 | tf_op jit(solution)/shard_map/all_gather | solution.py:299
  151.9 0.6 dynamic_slice.9
  152.4 0.1 concatenate.31
  152.5 0.6 pad_maximum_fusion.2.sm_ref
  153.2 26.4 %all-gather.8.cloned.1.call-done = bf16[3,3072,768]{2,1,0:T(8,128)(2,1)} async-done(((bf16[3,768,768]{2,1,0:T(8,128)(2,1)}), bf16[3,3072,768]{2,1,0:T(8,128)(2,1)}) %all-gather.8.cloned.1.call-update) | async-done | bytes 14155792 | tf_op jit(solution)/shard_map/all_gather | solution.py:297
  179.5 43.3 %forward.1 = (bf16[512,768]{1,0:T(8,128)(2,1)}, bf16[4,512,768]{2,1,0:T(8,128)(2,1)}, bf16[4,512,256]{2,1,0:T(8,128)(2,1)}, bf16[4,512,768]{2,1,0:T(8,128)(2,1)}...) custom-call(bf16[512,768]{1,0:T(8,128)(2,1)} %bitcast.61, ...), custom_call_target="tpu_custom_call" | custom-call | tf_op jit(solution)/shard_map/forward/pallas_call | solution.py:249
  222.8 47.6 %backward.1 = (bf16[512,768]{1,0:T(8,128)(2,1)}, bf16[3,4,768,768]{3,2,1,0:T(8,128)(2,1)}, f32[16,768]{1,0:T(8,128)}) custom-call(bf16[512,768]{1,0:T(8,128)(2,1)} %bitcast.62, s32[1,1]{1,0:T(1,128)} %bitcast.8.len_ref, bf16[3,4,768,768]{3,2,1,0:T(8,128)(2,1)} %bitcast.60, f32[16,768]{1,0:T(8,128)} %pad_maximum_fusion.2.sm_ref, ...), custom_call_target="tpu_custom_call" | custom-call | tf_op jit(solution)/shard_map/backward/pallas_call | solution.py:265
  270.5 0.2 reduce-scatter.5.cloned.1.call-start
  270.7 0.4 copy-done.7
  271.1 0.6 dynamic-slice
  271.7 243.8 %all-reduce.3.cloned.1.call-done = bf16[3,4,768,768]{3,2,1,0:T(8,128)(2,1)} async-done(((bf16[3,4,768,768]{3,2,1,0:T(8,128)(2,1)}), bf16[3,4,768,768]{3,2,1,0:T(8,128)(2,1)}) %all-reduce.3.cloned.1.call-update) | async-done | bytes 14155792
  515.5 4.6 dynamic-slice_bitcast_fusion
  520.2 1.1 copy-done.2
  521.3 1.2 copy.36
  522.5 0.5 broadcast.3
  523.0 5.4 reduce.7
  528.5 1.0 reshape.75
  529.5 3.5 all-to-all-start.3
  533.0 46.3 %psum.7 = f32[16,768]{1,0:T(8,128)S(1)} all-reduce(f32[16,768]{1,0:T(8,128)S(1)} %copy-done.3), channel_id=1, replica_groups=mesh['dp'=8,'tensor'=4] {'dp','tensor'}, use_global_device_ids=true, to_apply=%region_2.0 | all-reduce | flops 12288 | bytes 98304 | tf_op jit(solution)/shard_map/psum | solution.py:323
  579.3 1.2 copy.37
  580.5 5.4 reduce.6
  586.0 1.0 reshape.77
  587.0 3.5 all-to-all-start.2
  590.6 0.1 reshape.53
  590.7 0.1 reshape.54
  590.8 0.7 dynamic_slice.11
  591.4 0.7 fusion.1
  592.1 0.7 reshape.76
  592.9 1.2 copy.33
  594.1 8.0 %all-to-all-done.2 = bf16[4,2,49152]{2,1,0:T(2,128)(2,1)S(1)} async-done(((bf16[4,2,49152]{2,1,0:T(2,128)(2,1)}), bf16[4,2,49152]{2,1,0:T(2,128)(2,1)S(1)}, u32[]{:S(2)}, u32[]{:S(2)}) %all-to-all-start.2) | async-done | bytes 786464 | tf_op jit(solution)/shard_map/all_to_all | solution.py:314
  602.1 0.7 reshape.78
  602.9 1.0 copy.32
  603.9 1.1 convert_element_type.16
  605.0 0.9 slice_bitcast_fusion
  605.8 0.1 fusion.3
  606.0 0.7 copy.29
  606.7 0.7 pad_maximum_fusion.1
  (52 shorter events, 0.5 us)
Async XLA Ops:
  7.2 71.4 %copy-start = (bf16[4,128,768]{2,1,0:T(8,128)(2,1)S(1)}, bf16[4,128,768]{2,1,0:T(8,128)(2,1)}, u32[]{:S(2)}) copy-start(bf16[4,128,768]{2,1,0:T(8,128)(2,1)} %param.9) | copy-start | bytes 2359300
  7.2 71.4 %all-gather.6.cloned.1.call-start = ((), (), s32[]{:S(2)}) async-start(), calls=%async_computation.5 | async-start | bytes 3981312 | tf_op jit(solution)/shard_map/all_gather | solution.py:297
  11.1 168.5 %all-gather.8.cloned.1.call-start = ((), (), s32[]{:S(2)}) async-start(), calls=%async_computation.7 | async-start | bytes 17694720 | tf_op jit(solution)/shard_map/all_gather | solution.py:297
  78.5 20.8 %copy-start.4 = (bf16[8,96]{1,0:T(8,128)(2,1)S(1)}, bf16[8,96]{1,0:T(8,128)(2,1)}, u32[]{:S(2)}) copy-start(bf16[8,96]{1,0:T(8,128)(2,1)} %param.16) | copy-start | bytes 4612
  78.5 47.2 %copy-start.5 = (bf16[384]{0:T(512)(128)(2,1)S(1)}, bf16[384]{0:T(512)(128)(2,1)}, u32[]{:S(2)}) copy-start(bf16[384]{0:T(512)(128)(2,1)} %param.17) | copy-start | bytes 2308
  78.5 73.3 %copy-start.6 = (s32[4]{0:T(128)S(1)}, s32[4]{0:T(128)}, u32[]{:S(2)}) copy-start(s32[4]{0:T(128)} %param.10) | copy-start | bytes 52
  95.1 58.1 %all-to-all-start.1 = ((bf16[4,128,768]{2,1,0:T(8,128)(2,1)}), bf16[4,128,768]{2,1,0:T(8,128)(2,1)}, u32[]{:S(2)}, u32[]{:S(2)}) async-start(bf16[4,128,768]{2,1,0:T(8,128)(2,1)} %param.11), calls=%async_computation.1 | async-start | bytes 1572864 | tf_op jit(solution)/shard_map/all_to_all | solution.py:308
  99.3 416.2 %all-reduce.3.cloned.1.call-start = ((), (), s32[]{:S(2)}) async-start(), calls=%async_computation.8 | async-start | bytes 28311552
  270.5 0.7 copy-start.7
  270.5 333.4 %reduce-scatter.5.cloned.1.call-start = ((), (), s32[]{:S(2)}) async-start(), calls=%async_computation.6 | async-start | bytes 3981312 | tf_op jit(solution)/shard_map/reduce_scatter | solution.py:317
  520.1 1.1 copy-start.2
  522.5 10.5 %copy-start.3 = (f32[16,768]{1,0:T(8,128)S(1)}, f32[16,768]{1,0:T(8,128)}, u32[]{:S(2)}) copy-start(f32[16,768]{1,0:T(8,128)} %get-tuple-element.35) | copy-start | bytes 147460
  522.5 56.8 %copy-start.1 = (bf16[512,768]{1,0:T(8,128)(2,1)S(1)}, bf16[512,768]{1,0:T(8,128)(2,1)}, u32[]{:S(2)}) copy-start(bf16[512,768]{1,0:T(8,128)(2,1)} %get-tuple-element.22) | copy-start | bytes 2359300
  529.5 57.5 %all-to-all-start.3 = ((bf16[4,2,49152]{2,1,0:T(2,128)(2,1)}), bf16[4,2,49152]{2,1,0:T(2,128)(2,1)S(1)}, u32[]{:S(2)}, u32[]{:S(2)}) async-start(bf16[4,2,49152]{2,1,0:T(2,128)(2,1)} %reshape.75), calls=%async_computation.3 | async-start | bytes 1572864 | tf_op jit(solution)/shard_map/all_to_all | solution.py:315
  587.0 15.2 %all-to-all-start.2 = ((bf16[4,2,49152]{2,1,0:T(2,128)(2,1)}), bf16[4,2,49152]{2,1,0:T(2,128)(2,1)S(1)}, u32[]{:S(2)}, u32[]{:S(2)}) async-start(bf16[4,2,49152]{2,1,0:T(2,128)(2,1)} %reshape.77), calls=%async_computation.2 | async-start | bytes 1572864 | tf_op jit(solution)/shard_map/all_to_all | solution.py:314
Sparse Core Ops, SparseCore 0:
  11.2 67.3 all-gather.5
  80.1 99.3 all-gather.7
  270.6 244.8 all-reduce.2
  520.3 80.1 reduce-scatter.4

commit v2 on v1

--- a/solution.py
+++ b/solution.py
@@ -276,6 +276,364 @@
     )(x, length, w, sm, *saved, gsm)
 
 
+class Place:
+    def __init__(self, dp_count):
+        self.stride = dp_count // 8
+        dp_rank = lax.axis_index("dp")
+        tensor_rank = lax.axis_index("tensor")
+        group = dp_rank // self.stride
+        self.rest = dp_rank % self.stride
+        self.z, self.x = group // 2, group % 2
+        self.y, self.c = tensor_rank // 2, tensor_rank % 2
+
+    def device(self, z, x, y, c):
+        return ((z * 2 + x) * self.stride + self.rest, y * 2 + c)
+
+    def shifted(self, j, second, first, other=False):
+        if other:
+            second, first = first, second
+        across_x = self.c * second + (1 - self.c) * first
+        across_y = self.c * first + (1 - self.c) * second
+        return (self.z + j) % 4, (self.x + across_x) % 2, (self.y + across_y) % 2
+
+    def first(self):
+        return self.device(*self.shifted(0, 0, 1), self.c)
+
+    def second(self):
+        return self.device(*self.shifted(0, 1, 0), self.c)
+
+    def partner(self):
+        return self.device(self.z, self.x, self.y, 1 - self.c)
+
+    def along(self, j):
+        return self.device((self.z + j) % 4, self.x, self.y, self.c)
+
+    def in_tensor(self, r):
+        return self.device(self.z, self.x, (self.y + r // 2) % 2, (self.c + r % 2) % 2)
+
+    def in_dp(self, j, i):
+        return self.device((self.z + j) % 4, (self.x + i) % 2, self.y, self.c)
+
+
+def remote(src, dst, send, recv, device):
+    return pltpu.make_async_remote_copy(
+        src_ref=src, dst_ref=dst, send_sem=send, recv_sem=recv, device_id=device,
+        device_id_type=pl.DeviceIdType.MESH,
+    )
+
+
+def barrier(place):
+    sem = pltpu.get_barrier_semaphore()
+    peers = [place.in_dp(j, i) for j in range(4) for i in range(2) if j or i]
+    peers += [place.in_tensor(r) for r in range(1, 4)]
+    for peer in peers:
+        pl.semaphore_signal(sem, inc=1, device_id=peer, device_id_type=pl.DeviceIdType.MESH)
+    pl.semaphore_wait(sem, len(peers))
+
+
+class Gather:
+    def __init__(self, place, own, w, send, recv):
+        self.place, self.own, self.w, self.send, self.recv = place, own, w, send, recv
+        self.sent = []
+
+    def piece(self, k, s, f, j):
+        z, x, y = self.place.shifted(j, s, f)
+        return self.w.at[k, y * 2 + self.place.c, pl.ds(pl.multiple_of((z * 2 + x) * 96, 96), 96), :]
+
+    def push(self, k, src, dst, send, recv, device):
+        copy = remote(src, dst, self.send.at[k, send], self.recv.at[k, recv], device)
+        copy.start()
+        self.sent.append(copy)
+
+    def forward(self, k, s, f, j, to):
+        here = self.piece(k, s, f, j)
+        src = self.own.at[k] if (s, f, j) == (0, 0, 0) else here
+        if "f" in to:
+            self.push(k, src, here, 3 + j, 4 + j, self.place.first())
+        if "s" in to:
+            self.push(k, src, here, 7 + 4 * f + j, 8 + 4 * f + j, self.place.second())
+        if "p" in to:
+            self.push(k, src, here, 15 + 8 * s + 4 * f + j, 16 + 8 * s + 4 * f + j, self.place.partner())
+
+    def along(self, k):
+        for j in (1, 3, 2):
+            self.push(k, self.own.at[k], self.piece(k, 0, 0, 0), j - 1, 4 - j, self.place.along(j))
+
+    def wait(self, k, slot):
+        here = self.own.at[k]
+        remote(here, here, self.send.at[k, 0], self.recv.at[k, slot], self.place.partner()).wait_recv()
+
+    def relay(self, k, s, f, j):
+        self.wait(k, 8 * s + 4 * f + j)
+        self.forward(k, s, f, j, "p" if s else "sp" if f else "fsp")
+
+    def finish(self):
+        for copy in self.sent:
+            copy.wait_send()
+
+
+def gather_kernel(
+    dp_count, x_in, go_in, own, small_in,
+    w, x_out, go_out, small_out,
+    send, recv, local, tok_send, tok_recv, small_send, small_recv,
+):
+    place = Place(dp_count)
+    tensor_rank = lax.axis_index("tensor")
+    rows = pl.ds(pl.multiple_of(tensor_rank * 128, 128), 128)
+    barrier(place)
+    gather = Gather(place, own, w, send, recv)
+    copies = []
+    for i, (src, dst) in enumerate(((x_in, x_out), (go_in, go_out))):
+        here = pltpu.make_async_copy(src.at[tensor_rank], dst.at[rows, :], local.at[i])
+        here.start()
+        copies.append(here)
+    for k in range(3):
+        here = pltpu.make_async_copy(own.at[k], gather.piece(k, 0, 0, 0), local.at[2 + k])
+        here.start()
+        copies.append(here)
+    tokens = []
+    def send_tokens(i, src, dst):
+        for r in (2, 3, 1):
+            other = ((place.y + r // 2) % 2) * 2 + (place.c + r % 2) % 2
+            copy = remote(src.at[other], dst.at[rows, :], tok_send.at[i, r], tok_recv.at[i, r], place.in_tensor(r))
+            copy.start()
+            tokens.append(copy)
+    send_tokens(0, x_in, x_out)
+    here = pltpu.make_async_copy(small_in, small_out.at[0], local.at[5])
+    here.start()
+    copies.append(here)
+    for j in range(4):
+        for i in range(2):
+            if j or i:
+                slot = ((4 - j) % 4) * 2 + i
+                copy = remote(small_in, small_out.at[slot], small_send.at[slot], small_recv.at[slot], place.in_dp(j, i))
+                copy.start()
+                tokens.append(copy)
+    for k in range(3):
+        gather.along(k)
+        gather.forward(k, 0, 0, 0, "fsp")
+        if k == 1:
+            send_tokens(1, go_in, go_out)
+    for k in range(3):
+        for j in (1, 3, 2):
+            gather.relay(k, 0, 0, j)
+        for j in (0, 1, 3, 2):
+            gather.relay(k, 0, 1, j)
+        for f in range(2):
+            for j in (0, 1, 3, 2):
+                gather.relay(k, 1, f, j)
+    for k in range(3):
+        for slot in range(16, 32):
+            gather.wait(k, slot)
+    for copy in tokens:
+        copy.wait()
+    for copy in copies:
+        copy.wait()
+    gather.finish()
+
+
+def gather_call(dp_count, tokens, grad_out, own, small):
+    seq, width = tokens.shape[0] * tokens.shape[1], tokens.shape[2]
+    shapes = (((3, 4, width, 768), BF16), ((seq, width), BF16), ((seq, width), BF16), ((8, 16, width), BF16))
+    vmem = pl.BlockSpec(memory_space=pltpu.VMEM)
+    dma = pltpu.SemaphoreType.DMA
+    return pl.pallas_call(
+        functools.partial(gather_kernel, dp_count),
+        out_shape=[jax.ShapeDtypeStruct(s, d) for s, d in shapes],
+        in_specs=[vmem] * 4,
+        out_specs=[vmem] * 4,
+        scratch_shapes=[dma((3, 31)), dma((3, 32)), dma((6,)), dma((2, 4)), dma((2, 4)), dma((8,)), dma((8,))],
+        compiler_params=pltpu.CompilerParams(
+            vmem_limit_bytes=VMEM_LIMIT, collective_id=0, has_side_effects=True
+        ),
+        name="gather",
+    )(tokens, grad_out, own, small)
+
+
+class Scatter:
+    def __init__(self, place, g, inbox, out, send, recv):
+        self.place, self.g, self.inbox, self.out, self.send, self.recv = place, g, inbox, out, send, recv
+        self.sent = []
+
+    def piece(self, k, s, f, j, other=False):
+        z, x, y = self.place.shifted(j, s, f, other)
+        core = 1 - self.place.c if other else self.place.c
+        return (k, y * 2 + core, pl.multiple_of((z * 2 + x) * 96, 96))
+
+    def push(self, k, where, slot, device):
+        kind, t, row = where
+        copy = remote(
+            self.g.at[kind, t, pl.ds(row, 96), :], self.inbox.at[k, slot - 1],
+            self.send.at[k, slot - 1], self.recv.at[k, slot - 1], device,
+        )
+        copy.start()
+        self.sent.append(copy)
+
+    def to_partner(self, k, s, f):
+        for j in range(4):
+            self.push(k, self.piece(k, s, f, j, True), 16 + 8 * s + 4 * f + j, self.place.partner())
+
+    def wait(self, k, slot):
+        here = self.inbox.at[k, slot - 1]
+        remote(here, here, self.send.at[k, slot - 1], self.recv.at[k, slot - 1], self.place.partner()).wait_recv()
+
+    def add(self, k, s, f, j):
+        slots = [16 + 8 * s + 4 * f + j]
+        if not s:
+            slots.append(8 + 4 * f + j)
+        if not s and not f:
+            slots.append(4 + j)
+        last = (s, f, j) == (0, 0, 0)
+        if last:
+            slots += [1, 2, 3]
+        for slot in slots:
+            self.wait(k, slot)
+        kind, t, row = self.piece(k, s, f, j)
+
+        @pl.loop(0, 3)
+        def _(r):
+            lines = pl.ds(pl.multiple_of(row + r * 32, 32), 32)
+            total = self.g[kind, t, lines, :].astype(F32)
+            for slot in slots:
+                total += self.inbox[k, slot - 1, pl.ds(pl.multiple_of(r * 32, 32), 32), :].astype(F32)
+            if last:
+                self.out[k, pl.ds(pl.multiple_of(r * 32, 32), 32), :] = total
+            else:
+                self.g[kind, t, lines, :] = total.astype(BF16)
+
+        if last:
+            return
+        if s:
+            self.push(k, (kind, t, row), 8 + 4 * f + j, self.place.second())
+        elif f:
+            self.push(k, (kind, t, row), 4 + j, self.place.first())
+        else:
+            self.push(k, (kind, t, row), 4 - j, self.place.along(j))
+
+    def finish(self):
+        for copy in self.sent:
+            copy.wait_send()
+
+
+def sum_small(place, stages, inbox, out, send, recv):
+    hops = [(0, place.partner()), (1, place.second()), (2, place.first())]
+    sent = []
+    for i, peer in hops:
+        copy = remote(stages.at[i], inbox.at[i], send.at[i], recv.at[i], peer)
+        copy.start()
+        copy.wait_recv()
+        sent.append(copy)
+        stages[i + 1] = stages[i] + inbox[i]
+    for j in range(1, 4):
+        copy = remote(stages.at[3], inbox.at[6 - j], send.at[6 - j], recv.at[6 - j], place.along(j))
+        copy.start()
+        sent.append(copy)
+    for copy in sent[3:]:
+        copy.wait_recv()
+    out[...] = (stages[3] + inbox[3]) + (inbox[4] + inbox[5])
+    for copy in sent:
+        copy.wait_send()
+
+
+def scatter_kernel(
+    dp_count, out_in, gtok_in, grads, small_in,
+    output, gtok, shard, small,
+    g, inbox, stages, small_inbox, send, recv, local, tok_send, tok_recv, small_send, small_recv,
+):
+    place = Place(dp_count)
+    tensor_rank = lax.axis_index("tensor")
+    load = pltpu.make_async_copy(grads, g, local.at[2])
+    load.start()
+    barrier(place)
+    tokens = []
+    for i, (src, dst) in enumerate(((out_in, output), (gtok_in, gtok))):
+        for r in (2, 3, 1):
+            other = ((place.y + r // 2) % 2) * 2 + (place.c + r % 2) % 2
+            rows = pl.ds(pl.multiple_of(other * 128, 128), 128)
+            copy = remote(src.at[rows, :], dst.at[tensor_rank], tok_send.at[i, r], tok_recv.at[i, r], place.in_tensor(r))
+            copy.start()
+            tokens.append(copy)
+        rows = pl.ds(pl.multiple_of(tensor_rank * 128, 128), 128)
+        here = pltpu.make_async_copy(src.at[rows, :], dst.at[tensor_rank], local.at[i])
+        here.start()
+        tokens.append(here)
+    load.wait()
+    scatter = Scatter(place, g, inbox, shard, send, recv)
+    for k in (2, 1, 0):
+        for s in (1, 0):
+            for f in (1, 0):
+                scatter.to_partner(k, s, f)
+    stages[0] = small_in[...]
+    sum_small(place, stages, small_inbox, small, small_send, small_recv)
+    order = (2, 1, 0)
+    for k in order:
+        for f in (1, 0):
+            for j in (2, 1, 3, 0):
+                scatter.add(k, 1, f, j)
+    for k in order:
+        for j in (2, 1, 3, 0):
+            scatter.add(k, 0, 1, j)
+    for k in order:
+        for j in (2, 1, 3):
+            scatter.add(k, 0, 0, j)
+    for k in order:
+        scatter.add(k, 0, 0, 0)
+    for copy in tokens:
+        copy.wait()
+    scatter.finish()
+
+
+def scatter_call(dp_count, out, gtok, grads, small):
+    seq, width = out.shape
+    shapes = (((4, seq // 4, width), BF16), ((4, seq // 4, width), BF16), ((3, 96, width), F32), ((16, width), F32))
+    vmem = pl.BlockSpec(memory_space=pltpu.VMEM)
+    dma = pltpu.SemaphoreType.DMA
+    return pl.pallas_call(
+        functools.partial(scatter_kernel, dp_count),
+        out_shape=[jax.ShapeDtypeStruct(s, d) for s, d in shapes],
+        in_specs=[vmem, vmem, pl.BlockSpec(memory_space=pl.ANY), vmem],
+        out_specs=[vmem] * 4,
+        scratch_shapes=[
+            pltpu.VMEM(grads.shape, BF16), pltpu.VMEM((3, 31, 96, width), BF16),
+            pltpu.VMEM((4, 16, width), F32), pltpu.VMEM((6, 16, width), F32),
+            dma((3, 31)), dma((3, 31)), dma((3,)), dma((2, 4)), dma((2, 4)), dma((6,)), dma((6,)),
+        ],
+        compiler_params=pltpu.CompilerParams(
+            vmem_limit_bytes=VMEM_LIMIT, collective_id=1, has_side_effects=True
+        ),
+        name="scatter",
+    )(out, gtok, grads, small)
+
+
+def gather_groups(shard, dp_count, axis):
+    stride = dp_count // 8
+    if stride == 1:
+        return shard
+    groups = [[g * stride + i for i in range(stride)] for g in range(8)]
+    return lax.all_gather(shard, "dp", axis=axis, tiled=True, axis_index_groups=groups)
+
+
+def scatter_groups(shard, small, dp_count):
+    stride = dp_count // 8
+    if stride == 1:
+        return shard, small
+    groups = [[g * stride + i for i in range(stride)] for g in range(8)]
+    shard = lax.psum_scatter(shard, "dp", scatter_dimension=1, tiled=True, axis_index_groups=groups)
+    return shard, lax.psum(small, "dp", axis_index_groups=groups)
+
+
+def pack_small(vectors, bias, dp_count, width):
+    group = lax.axis_index("dp") // (dp_count // 8)
+    part = vectors.shape[1]
+    rows = lax.dynamic_update_slice(jnp.zeros((8, width), BF16), vectors, (0, group * part))
+    units = lax.dynamic_update_slice(jnp.zeros((4 * width,), BF16), bias, (group * (4 * part),))
+    qb = rows[0].reshape(4, 192)
+    vb = rows[1].reshape(4, 192)
+    none = jnp.zeros((4, 128), BF16)
+    packed = jnp.concatenate([qb[:, :128], none, vb[:, :128], qb[:, 128:], none, vb[:, 128:], none], axis=1)
+    return jnp.concatenate([rows, units.reshape(4, width), packed], axis=0)
+
+
 def pack_attention(q, k, v, o):
     return jnp.concatenate(
         [q[:, :128], k[:, :128], v[:, :128], q[:, 128:], k[:, 128:], o[:, 128:], v[:, 128:], o[:, :128]], axis=1
@@ -294,33 +652,23 @@
     own = jnp.stack([
         pack_attention(qkv_weight[0], qkv_weight[1], qkv_weight[2], out_weight.T), up_weight, down_weight.T
     ])
-    w = lax.all_gather(lax.all_gather(own, "dp", axis=1, tiled=True), "tensor", axis=1)
-    vec = lax.all_gather(vectors, "dp", axis=1, tiled=True).astype(F32)
-    hb = lax.all_gather(hidden_bias, "dp", axis=0, tiled=True).astype(F32).reshape(4, 768)
-    qb = vec[0].reshape(4, 192)
-    vb = vec[1].reshape(4, 192)
-    none = jnp.zeros((4, 128), F32)
-    qkvb = jnp.concatenate(
-        [qb[:, :128], none, vb[:, :128], qb[:, 128:], none, vb[:, 128:], none], axis=1
-    )
-    sm = jnp.concatenate([vec, hb, qkvb], axis=0)
-    x = lax.all_to_all(tokens, "tensor", 0, 1, tiled=True)[0]
-    go = lax.all_to_all(grad_out, "tensor", 0, 1, tiled=True)[0]
+    own = gather_groups(own, dp_count, 1)
+    small = pack_small(gather_groups(vectors, dp_count, 1), gather_groups(hidden_bias, dp_count, 0), dp_count, width)
+    w, x, go, smalls = gather_call(dp_count, tokens, grad_out, own, small)
+    sm = jnp.sum(smalls.astype(F32), axis=0)
     length = lax.dynamic_slice_in_dim(lengths, tensor_rank, 1).reshape(1, 1)
 
     out, *saved, gsm = forward_call(x, go, length, w, sm)
     gtok, grads, gsm = backward_call(x, length, w, sm, saved, gsm)
 
-    output = lax.all_to_all(out[None], "tensor", 1, 0, tiled=True)
-    grad_tokens = lax.all_to_all(gtok[None], "tensor", 1, 0, tiled=True).astype(F32)
-    g = lax.psum_scatter(grads, "tensor", scatter_dimension=1)
-    g = lax.psum_scatter(g, "dp", scatter_dimension=1, tiled=True).astype(F32)
+    output, gtok, g, gsm = scatter_call(dp_count, out, gtok, grads, gsm)
+    grad_tokens = gtok.astype(F32)
+    g, gsm = scatter_groups(g, gsm, dp_count)
     a = g[0]
     gq = jnp.concatenate([a[:, 0:128], a[:, 384:448]], axis=1)
     gk = jnp.concatenate([a[:, 128:256], a[:, 448:512]], axis=1)
     gv = jnp.concatenate([a[:, 256:384], a[:, 576:640]], axis=1)
     gout = jnp.concatenate([a[:, 640:768], a[:, 512:576]], axis=1).T
-    gsm = lax.psum(gsm, ("dp", "tensor"))
     packed = gsm[12:16]
     row_q = jnp.concatenate([packed[:, 0:128], packed[:, 384:448]], axis=1).reshape(1, width)
     row_v = jnp.concatenate([packed[:, 256:384], packed[:, 576:640]], axis=1).reshape(1, width)

time: 615 us -> 321 us (0.52)
  waiting for transfers between devices: 346 us -> 0 us
  Pallas kernels: 90.9 us -> 302 us
  blocking collectives: 115 us -> 0 us
  between operations: 14.1 us -> 0.8 us
  starting transfers between devices: 11.6 us -> 0 us
  local copies, waits for them, and re-layouts: 20.9 us -> 9.78 us
  other arithmetic: 15.8 us -> 7.93 us
    unnamed x5 -> x0, waiting for transfers between devices: 244 us -> none
    pallas_call x0 -> x2, Pallas kernels: none -> 211 us  [the longest x1 115 us: scatter_call(): pl.pallas_call(functools.partial(scatter_kernel, dp_count), out_shape=[ja...]
    all_gather x2 -> x0, waiting for transfers between devices: 93.8 us -> none  [the longest x1 67.4 us: shards(): lax.all_gather(own, 'dp', axis=1, tiled=True)]
    all_gather x2 -> x0, blocking collectives: 52.1 us -> none  [the longest x1 26.1 us: shards(): vec = lax.all_gather(vectors, 'dp', axis=1, tiled=True).astype(F32)]
    psum x1 -> x0, blocking collectives: 46.3 us -> none  [shards(): gsm = lax.psum(gsm, ('dp', 'tensor'))]
    all_to_all x1 -> x0, blocking collectives: 16.5 us -> none  [shards(): x = lax.all_to_all(tokens, 'tensor', 0, 1, tiled=True)[0]]
    all_to_all x3 -> x0, starting transfers between devices: 11.2 us -> none  [the longest x1 4.2 us: shards(): go = lax.all_to_all(grad_out, 'tensor', 0, 1, tiled=True)[0]]
    unnamed x2 -> x0, other arithmetic: 10.9 us -> none
  transfers between devices with their start and end apart: 7 -> 0, of which waited for: 4 -> 0; matrix products, arithmetic and copies ran while one was open for 4% -> 0% of each run, Pallas kernels for 0% -> 0%
where the time goes in v2:
time: 321 us; the launch traced here: 320 us
  Pallas kernels  302 us (94%)
  local copies, waits for them, and re-layouts  9.78 us (3%)
  other arithmetic  7.93 us (2%)
    pallas_call x1, Pallas kernels, scatter_call(): pl.pallas_call(functools.partial(scatter_kernel, dp_count), out_shape=[ja...  115 us
    pallas_call x1, Pallas kernels, gather_call(): pl.pallas_call(functools.partial(gather_kernel, dp_count), out_shape=[jax...  95.7 us
    pallas_call x1, Pallas kernels, backward_call(): pl.pallas_call(backward_kernel, out_shape=[jax.ShapeDtypeStruct(s, d) for...  47.6 us
    pallas_call x1, Pallas kernels, forward_call(): pl.pallas_call(forward_kernel, out_shape=[jax.ShapeDtypeStruct(s, d) for...  43.3 us

profile of v2, /device:TPU:0, one launch (start us, length us, event | category | flops | bytes accessed | tf_op | source)
XLA Modules:
  0.0 320.2 jit_solution(3399018184307046598)
XLA Ops:
  0.6 0.9 slice_bitcast_fusion.3
  1.6 0.9 copy.17
  2.5 0.1 concatenate.30
  2.6 1.8 pad_maximum_fusion.own
  4.4 0.8 dynamic_update_slice.6
  5.2 0.1 reshape_squeeze.6
  5.3 0.1 reshape_squeeze.7
  5.4 0.1 concatenate.31
  5.5 0.9 dynamic_update_slice.7
  6.4 0.6 pad_maximum_fusion.2.small_in
  7.0 95.7 %gather.1 = (bf16[3,4,768,768]{3,2,1,0:T(8,128)(2,1)}, bf16[512,768]{1,0:T(8,128)(2,1)}, bf16[512,768]{1,0:T(8,128)(2,1)}, bf16[8,16,768]{2,1,0:T(8,128)(2,1)}) custom-call(bf16[4,128,768]{2,1,0:T(8,128)(2,1)} %x_in.1, bf16[4,128,768]{2,1,0:T(8,128)(2,1)} %go_in.1, bf16[3,96,768]{2,1,0:T(8,128)(2,1)} %pad_maximum_fusion.own, ...), custom_call_target="tpu_custom_call" | custom-call | tf_op jit(solution)/shard_map/gather/pallas_call | solution.py:440
  102.7 1.2 dynamic_slice.9
  103.9 1.6 convert_reduce_fusion.sm_ref
  105.5 43.3 %forward.1 = (bf16[512,768]{1,0:T(8,128)(2,1)}, bf16[4,512,768]{2,1,0:T(8,128)(2,1)}, bf16[4,512,256]{2,1,0:T(8,128)(2,1)}, bf16[4,512,768]{2,1,0:T(8,128)(2,1)}...) custom-call(bf16[512,768]{1,0:T(8,128)(2,1)} %get-tuple-element.30.x, ...), custom_call_target="tpu_custom_call" | custom-call | tf_op jit(solution)/shard_map/forward/pallas_call | solution.py:249
  148.8 47.6 %backward.1 = (bf16[512,768]{1,0:T(8,128)(2,1)}, bf16[3,4,768,768]{3,2,1,0:T(8,128)(2,1)}, f32[16,768]{1,0:T(8,128)}) custom-call(bf16[512,768]{1,0:T(8,128)(2,1)} %get-tuple-element.30.x_ref, s32[1,1]{1,0:T(1,128)} %bitcast.8.len_ref, bf16[3,4,768,768]{3,2,1,0:T(8,128)(2,1)} %get-tuple-element.32.w_ref, f32[16,768]{1,0:T(8,128)} %convert_reduce_fusion.sm_ref, ...), custom_call_target="tpu_custom_call" | custom-call | tf_op jit(solution)/shard_map/backward/pallas_call | solution.py:265
  196.4 115.1 %scatter.1 = (bf16[4,128,768]{2,1,0:T(8,128)(2,1)}, bf16[4,128,768]{2,1,0:T(8,128)(2,1)}, f32[3,96,768]{2,1,0:T(8,128)}, f32[16,768]{1,0:T(8,128)}) custom-call(bf16[512,768]{1,0:T(8,128)(2,1)} %get-tuple-element.34.out_in, bf16[512,768]{1,0:T(8,128)(2,1)} %get-tuple-element.45.gtok_in, bf16[3,4,768,768]{3,2,1,0:T(8,128)(2,1)} %get-tuple-element.46.grads, ...), custom_call_target="tpu_custom_call" | custom-call | tf_op jit(solution)/shard_map/scatter/pallas_call | solution.py:591
  311.6 0.0 copy-start.1
  311.6 0.0 copy-start
  311.6 2.5 convert_element_type.7
  314.1 2.0 slice_bitcast_fusion
  316.1 0.1 fusion.3
  316.2 0.7 pad_maximum_fusion.1
  317.0 0.7 copy.18
  317.7 0.0 copy-done.1
  317.7 0.1 fusion.5
  317.8 0.1 reshape.33
  317.9 0.1 reshape.34
  318.0 0.7 fusion.1
  318.7 0.7 dynamic_slice.11
  319.3 0.0 copy-done
  319.3 0.9 copy.22
  (26 shorter events, 0.2 us)
Async XLA Ops:
  311.6 6.2 %copy-start.1 = (f32[16,768]{1,0:T(8,128)S(1)}, f32[16,768]{1,0:T(8,128)}, u32[]{:S(2)}) copy-start(f32[16,768]{1,0:T(8,128)} %get-tuple-element.51) | copy-start | bytes 147460
  311.6 7.8 %copy-start = (bf16[4,128,768]{2,1,0:T(8,128)(2,1)S(1)}, bf16[4,128,768]{2,1,0:T(8,128)(2,1)}, u32[]{:S(2)}) copy-start(bf16[4,128,768]{2,1,0:T(8,128)(2,1)} %get-tuple-element.92) | copy-start | bytes 2359300

commit v3 on v1

v3 whole, which is shorter than its diff:
```python
import functools

import jax
import jax.numpy as jnp
import numpy as np
from jax import lax
from jax.experimental import pallas as pl
from jax.experimental.pallas import tpu as pltpu
from jax.sharding import PartitionSpec as P

HD = 64
EPS = 1e-12
NEG = -1e30
F32 = jnp.float32
BF16 = jnp.bfloat16
VMEM_LIMIT = 67043328
ROWS = 128


def dot(left, right):
    return lax.dot_general(left, right, (((1,), (0,)), ((), ())), preferred_element_type=F32)


def dot_nt(left, right):
    return lax.dot_general(left, right, (((1,), (1,)), ((), ())), preferred_element_type=F32)


def lane_masks(scale):
    lane = lax.broadcasted_iota(jnp.int32, (1, 128), 1)
    low = jnp.where(lane < HD, F32(scale), F32(0)).astype(BF16)
    high = jnp.where(lane < HD, F32(0), F32(scale)).astype(BF16)
    return low, high


def is_low(shape):
    return lax.broadcasted_iota(jnp.int32, shape, 1) < HD


def put_row(ref, row, span, value):
    old = ref[8:16, span]
    here = lax.broadcasted_iota(jnp.int32, old.shape, 0) == row
    ref[8:16, span] = jnp.where(here, value, old)


class Place:
    def __init__(self, dp_count):
        self.stride = dp_count // 8
        dp_rank = lax.axis_index("dp")
        tensor_rank = lax.axis_index("tensor")
        group = dp_rank // self.stride
        self.rest = dp_rank % self.stride
        self.z, self.x = group // 2, group % 2
        self.y, self.c = tensor_rank // 2, tensor_rank % 2

    def device(self, z, x, y, c):
        return ((z * 2 + x) * self.stride + self.rest, y * 2 + c)

    def shifted(self, j, second, first, other=False):
        if other:
            second, first = first, second
        across_x = self.c * second + (1 - self.c) * first
        across_y = self.c * first + (1 - self.c) * second
        return (self.z + j) % 4, (self.x + across_x) % 2, (self.y + across_y) % 2

    def first(self):
        return self.device(*self.shifted(0, 0, 1), self.c)

    def second(self):
        return self.device(*self.shifted(0, 1, 0), self.c)

    def partner(self):
        return self.device(self.z, self.x, self.y, 1 - self.c)

    def along(self, j):
        return self.device((self.z + j) % 4, self.x, self.y, self.c)

    def in_tensor(self, r):
        return self.device(self.z, self.x, (self.y + r // 2) % 2, (self.c + r % 2) % 2)

    def in_dp(self, j, i):
        return self.device((self.z + j) % 4, (self.x + i) % 2, self.y, self.c)


def remote(src, dst, send, recv, device):
    return pltpu.make_async_remote_copy(
        src_ref=src, dst_ref=dst, send_sem=send, recv_sem=recv, device_id=device,
        device_id_type=pl.DeviceIdType.MESH,
    )


def barrier(place):
    sem = pltpu.get_barrier_semaphore()
    peers = [place.in_dp(j, i) for j in range(4) for i in range(2) if j or i]
    peers += [place.in_tensor(r) for r in range(1, 4)]
    for peer in peers:
        pl.semaphore_signal(sem, inc=1, device_id=peer, device_id_type=pl.DeviceIdType.MESH)
    pl.semaphore_wait(sem, len(peers))


class Gather:
    def __init__(self, place, own, w, send, recv):
        self.place, self.own, self.w, self.send, self.recv = place, own, w, send, recv

    def piece(self, k, s, f, j):
        z, x, y = self.place.shifted(j, s, f)
        return self.w.at[k, y * 2 + self.place.c, pl.ds(pl.multiple_of((z * 2 + x) * 96, 96), 96), :]

    def push(self, k, src, dst, send, recv, device):
        remote(src, dst, self.send.at[k, send], self.recv.at[k, recv], device).start()

    def forward(self, k, s, f, j, to):
        here = self.piece(k, s, f, j)
        src = self.own.at[k] if (s, f, j) == (0, 0, 0) else here
        if "f" in to:
            self.push(k, src, here, 3 + j, 4 + j, self.place.first())
        if "s" in to:
            self.push(k, src, here, 7 + 4 * f + j, 8 + 4 * f + j, self.place.second())
        if "p" in to:
            self.push(k, src, here, 15 + 8 * s + 4 * f + j, 16 + 8 * s + 4 * f + j, self.place.partner())

    def along(self, k):
        for j in (1, 3, 2):
            self.push(k, self.own.at[k], self.piece(k, 0, 0, 0), j - 1, 4 - j, self.place.along(j))

    def start(self, k):
        self.forward(k, 0, 0, 0, "fsp")

    def wait(self, k, slot):
        here = self.own.at[k]
        remote(here, here, self.send.at[k, 0], self.recv.at[k, slot], self.place.partner()).wait_recv()

    def relay(self, k, s, f, order):
        for j in order:
            self.wait(k, 8 * s + 4 * f + j)
            self.forward(k, s, f, j, "p" if s else "sp" if f else "fsp")

    def others(self, k):
        @pl.loop(16, 32)
        def _(slot):
            self.wait(k, slot)

    def finish(self):
        for k in range(3):
            here = self.own.at[k]

            @pl.loop(0, 31)
            def _(slot):
                remote(here, here, self.send.at[k, slot], self.recv.at[k, 1], self.place.partner()).wait_send()


class Scatter:
    def __init__(self, place, g, boxes, sends, recvs, out):
        self.place, self.g, self.boxes, self.sends, self.recvs, self.out = place, g, boxes, sends, recvs, out

    def push(self, stage, src, index, sem, device):
        remote(
            src, self.boxes[stage].at[index], self.sends[stage].at[sem], self.recvs[stage].at[sem], device
        ).start()

    def piece(self, k, s, f, j):
        z, x, y = self.place.shifted(j, s, f)
        return k, y * 2 + self.place.c, pl.multiple_of((z * 2 + x) * 96, 96)

    def view(self, k, s, f, j):
        kind, t, row = self.piece(k, s, f, j)
        return self.g.at[kind, t, pl.ds(row, 96), :]

    def wait(self, stage, index, sem):
        here = self.boxes[stage].at[index]
        remote(here, here, self.sends[stage].at[sem], self.recvs[stage].at[sem], self.place.partner()).wait_recv()

    def to_partner(self, k, t, i):
        self.push(0, self.g.at[k, t], (k, i), (k, i), self.place.partner())

    def from_partner(self, k, i):
        self.wait(0, (k, i), (k, i))

    def across(self, k, f):
        for j in (2, 1, 3, 0):
            self.push(1, self.view(k, 1, f, j), (k, f, j), (k, 4 * f + j), self.place.second())

    def ready(self, k, i):
        if i == 0:
            self.across(k, 1)

            @pl.when(self.place.c == 0)
            def _():
                self.across(k, 0)
        else:
            @pl.when(self.place.c == 1)
            def _():
                self.across(k, 0)

    def total(self, k, f, j, parts, last=False):
        kind, t, row = self.piece(k, 0, f, j)

        @pl.loop(0, 3)
        def _(r):
            lines = pl.ds(pl.multiple_of(row + r * 32, 32), 32)
            local = pl.ds(pl.multiple_of(r * 32, 32), 32)
            value = self.g[kind, t, lines, :].astype(F32)
            for stage, index in parts:
                value += self.boxes[stage][(*index, local, slice(None))].astype(F32)
            if last:
                self.out[k, local, :] = value
            else:
                self.g[kind, t, lines, :] = value.astype(BF16)

    def add_far(self, k):
        for j in (2, 1, 3, 0):
            self.wait(1, (k, 1, j), (k, 4 + j))
            self.total(k, 1, j, [(1, (k, 1, j))])
            self.push(2, self.view(k, 0, 1, j), (k, j), (k, j), self.place.first())

    def add_near(self, k):
        for j in (2, 1, 3):
            self.wait(1, (k, 0, j), (k, j))
            self.wait(2, (k, j), (k, j))
            self.total(k, 0, j, [(1, (k, 0, j)), (2, (k, j))])
            self.push(3, self.view(k, 0, 0, j), (k, 3 - j), (k, 3 - j), self.place.along(j))

    def add_last(self, k):
        self.wait(1, (k, 0, 0), (k, 0))
        self.wait(2, (k, 0), (k, 0))
        for i in range(3):
            self.wait(3, (k, i), (k, i))
        self.total(k, 0, 0, [(1, (k, 0, 0)), (2, (k, 0)), (3, (k, 0)), (3, (k, 1)), (3, (k, 2))], True)

    def finish(self):
        counts = ((0, 2), (1, 8), (2, 4), (3, 3))
        for k in range(3):
            for stage, count in counts:
                here = self.g.at[0, 0] if stage == 0 else self.boxes[2].at[0, 0]

                @pl.loop(0, count)
                def _(i):
                    remote(
                        here, here, self.sends[stage].at[k, i], self.recvs[stage].at[k, i], self.place.partner()
                    ).wait_send()


class SmallSum:
    def __init__(self, place, stages, inbox, send, recv):
        self.place, self.stages, self.inbox, self.send, self.recv = place, stages, inbox, send, recv
        self.sent = []

    def push(self, stage, slot, peer):
        copy = remote(self.stages.at[stage], self.inbox.at[slot], self.send.at[slot], self.recv.at[slot], peer)
        copy.start()
        self.sent.append(copy)

    def start(self, i):
        if i < 3:
            self.push(i, i, (self.place.partner, self.place.second, self.place.first)[i]())
        else:
            for j in range(1, 4):
                self.push(3, 6 - j, self.place.along(j))

    def step(self, i):
        self.sent[i].wait_recv()
        self.stages[i + 1] = self.stages[i] + self.inbox[i]
        self.start(i + 1)

    def finish(self, out):
        for copy in self.sent[3:]:
            copy.wait_recv()
        out[...] = (self.stages[3] + self.inbox[3]) + (self.inbox[4] + self.inbox[5])
        for copy in self.sent:
            copy.wait_send()


class Tokens:
    def __init__(self, place, send, recv, local):
        self.place, self.send, self.recv, self.local = place, send, recv, local
        self.rank = place.y * 2 + place.c

    def other(self, r):
        return ((self.place.y + r // 2) % 2) * 2 + (self.place.c + r % 2) % 2

    def rows(self, rank):
        return pl.ds(pl.multiple_of(rank * 128, 128), 128)

    def gather(self, i, src, dst):
        here = dst.at[self.rows(self.rank), :]
        pltpu.make_async_copy(src.at[self.rank], here, self.local.at[i]).start()
        for r in (2, 3, 1):
            remote(
                src.at[self.other(r)], here, self.send.at[i, r], self.recv.at[i, r], self.place.in_tensor(r)
            ).start()

    def spread(self, i, src, dst):
        here = dst.at[self.rank]
        pltpu.make_async_copy(src.at[self.rows(self.rank), :], here, self.local.at[i]).start()
        for r in (2, 3, 1):
            remote(
                src.at[self.rows(self.other(r)), :], here, self.send.at[i, r], self.recv.at[i, r],
                self.place.in_tensor(r),
            ).start()

    def wait(self, i, block, arrive=True, leave=True):
        for r in (1, 2, 3):
            copy = remote(block, block, self.send.at[i, r], self.recv.at[i, r], self.place.in_tensor(r))
            if arrive:
                copy.wait_recv()
            if leave:
                copy.wait_send()
        if arrive:
            pltpu.make_async_copy(block, block, self.local.at[i]).wait()


def layer_kernel(
    dp_count, x_in, go_in, own, small_in, len_ref,
    output, gtok, shard, small,
    w, x, go, smalls, sm, qkv, ctx, act, gp, hb, n1, s1, g2, stat, gsm,
    acc, pre, low_grad, tall, gpre, gctx, gpacked,
    box_p, box_s, box_f, box_z, stages, small_box,
    send, recv, tok_send, tok_recv, tok_local, own_local, bias_send, bias_recv,
    send_p, recv_p, send_s, recv_s, send_f, recv_f, send_z, recv_z, small_send, small_recv,
):
    seq, width = x.shape
    blocks = seq // ROWS
    place = Place(dp_count)
    gather = Gather(place, own, w, send, recv)
    tokens = Tokens(place, tok_send, tok_recv, tok_local)
    near = (0, 1, 3, 2)
    line = (1, 3, 2)

    barrier(place)
    gather.along(0)
    gather.start(0)
    tokens.gather(0, x_in, x)
    for k in range(3):
        pltpu.make_async_copy(own.at[k], gather.piece(k, 0, 0, 0), own_local.at[k]).start()
    pltpu.make_async_copy(small_in, smalls.at[0], own_local.at[3]).start()
    for j in range(4):
        for i in range(2):
            if j or i:
                slot = ((4 - j) % 4) * 2 + i
                remote(
                    small_in, smalls.at[slot], bias_send.at[slot], bias_recv.at[slot], place.in_dp(j, i)
                ).start()
    gather.along(1)
    gather.start(1)
    gather.along(2)
    gather.relay(0, 0, 0, line)
    gather.relay(0, 0, 1, near)
    gather.relay(0, 1, 0, near)
    gather.relay(1, 0, 0, line)
    gather.relay(0, 1, 1, near)
    gather.start(2)
    for k in range(3):
        pltpu.make_async_copy(own.at[k], own.at[k], own_local.at[k]).wait()
    pltpu.make_async_copy(small_in, small_in, own_local.at[3]).wait()

    @pl.loop(1, 8)
    def _(slot):
        remote(small_in, small_in, bias_send.at[slot], bias_recv.at[slot], place.partner()).wait()

    total = smalls[0].astype(F32)
    for i in range(1, 8):
        total += smalls[i].astype(F32)
    sm[...] = total
    tokens.wait(0, x_in.at[0])
    gather.others(0)

    low, high = lane_masks(0.125)
    length = len_ref[0, 0]
    key_bias = jnp.where(lax.broadcasted_iota(jnp.int32, (1, seq), 1) < length, F32(0), F32(NEG))
    acc[...] = jnp.zeros_like(acc)

    attention_events = {
        0: lambda: gather.relay(1, 0, 1, (0, 1)),
        1: lambda: gather.relay(1, 0, 1, (3, 2)),
        2: lambda: gather.relay(2, 0, 0, line),
        3: lambda: gather.relay(1, 1, 0, near),
        4: lambda: tokens.gather(1, go_in, go),
        5: lambda: gather.relay(1, 1, 1, near),
        6: lambda: gather.relay(2, 0, 1, (0, 1)),
        7: lambda: gather.relay(2, 0, 1, (3, 2)),
    }

    @pl.loop(0, 4)
    def _(t):
        proj = dot(x[...], w[0, t, :, 0:640]) + sm[pl.ds(12 + t, 1), 0:640]
        qkv[t, :, 0:640] = proj.astype(BF16)
        q_two = pltpu.roll(jnp.where(is_low((seq, 128)), proj[:, 384:512] * 0.125, 0.0), 64, 1)
        qkv[t, :, 640:768] = q_two.astype(BF16)

        @pl.loop(0, seq // 256)
        def _(r):
            for slot, event in attention_events.items():
                pl.when(t * 2 + r == slot)(event)
            rows = pl.ds(pl.multiple_of(r * 256, 256), 256)
            q_pair = qkv[t, rows, 0:128]
            outs = []
            stats = []
            for h in range(3):
                if h < 2:
                    queries = q_pair * (low, high)[h]
                    keys = qkv[t, :, 128:256]
                    values = qkv[t, :, 256:384]
                else:
                    queries = qkv[t, rows, 640:768]
                    keys = qkv[t, :, 384:512]
                    values = qkv[t, :, 512:640]
                scores = dot_nt(queries, keys) + key_bias
                highest = jnp.max(scores, axis=1, keepdims=True)
                grown = jnp.exp(scores - highest)
                total = jnp.sum(grown, axis=1, keepdims=True)
                probs = (grown * (1.0 / total)).astype(BF16)
                outs.append(dot(probs, values))
                stats.append(highest + jnp.log(total))
            lowest = is_low((256, 128))
            ctx[t, rows, 0:128] = jnp.where(lowest, pltpu.roll(outs[2], 64, 1), 0.0).astype(BF16)
            ctx[t, rows, 128:256] = jnp.where(lowest, outs[0], outs[1]).astype(BF16)
            lane = lax.broadcasted_iota(jnp.int32, (256, 128), 1)
            stat[t, rows, :] = jnp.where(lane == 0, stats[0], jnp.where(lane == 1, stats[1], stats[2]))

        acc[...] += dot_nt(ctx[t], w[0, t, :, 512:768])

    @pl.loop(0, blocks)
    def _(r):
        rows = pl.ds(pl.multiple_of(r * ROWS, ROWS), ROWS)
        resid = x[rows, :].astype(F32) + acc[rows, :] + sm[2:3, :]
        centred = resid - jnp.mean(resid, axis=1, keepdims=True)
        scale = lax.rsqrt(jnp.mean(centred * centred, axis=1, keepdims=True) + EPS)
        normed = centred * scale
        hidden = normed * sm[3:4, :] + sm[4:5, :]
        n1[rows, :] = normed
        s1[rows, :] = jnp.broadcast_to(scale, (ROWS, 128))
        hb[rows, :] = hidden.astype(BF16)
        acc[rows, :] = hidden + sm[5:6, :]

    gather.relay(2, 1, 0, (0, 1))
    gather.others(1)
    up_events = {
        1: lambda: gather.relay(2, 1, 0, (3, 2)),
        2: lambda: gather.relay(2, 1, 1, (0, 1)),
        3: lambda: gather.relay(2, 1, 1, (3, 2)),
    }

    @pl.loop(0, 4)
    def _(t):
        for slot, event in up_events.items():
            pl.when(t == slot)(event)
        pre[...] = dot(hb[...], w[1, t])

        @pl.loop(0, blocks)
        def _(r):
            rows = pl.ds(pl.multiple_of(r * ROWS, ROWS), ROWS)
            u = pre[rows, :] + sm[pl.ds(8 + t, 1), :]
            cdf = 0.5 + 0.5 * lax.erf(u * F32(np.sqrt(0.5)))
            density = jnp.exp(u * u * -0.5) * F32(1.0 / np.sqrt(2.0 * np.pi))
            act[t, rows, :] = (u * cdf).astype(BF16)
            gp[t, rows, :] = (cdf + u * density).astype(BF16)

    gather.others(2)

    @pl.loop(0, 4)
    def _(t):
        acc[...] += dot_nt(act[t], w[2, t])

    tokens.wait(1, x_in.at[0])
    gsm[...] = jnp.zeros_like(gsm)

    @pl.loop(0, blocks)
    def _(r):
        rows = pl.ds(pl.multiple_of(r * ROWS, ROWS), ROWS)
        resid = acc[rows, :]
        centred = resid - jnp.mean(resid, axis=1, keepdims=True)
        scale = lax.rsqrt(jnp.mean(centred * centred, axis=1, keepdims=True) + EPS)
        normed = centred * scale
        gain = sm[6:7, :]
        cot = go[rows, :].astype(F32)
        go[rows, :] = (normed * gain + sm[7:8, :]).astype(BF16)
        e = cot * gain
        en = jnp.mean(e * normed, axis=1, keepdims=True)
        grad = scale * (e - jnp.mean(e, axis=1, keepdims=True) - normed * en)
        g2[rows, :] = grad
        gsm[5:6, :] += jnp.sum(grad, axis=0, keepdims=True)
        gsm[6:7, :] += jnp.sum(cot * normed, axis=0, keepdims=True)
        gsm[7:8, :] += jnp.sum(cot, axis=0, keepdims=True)

    tokens.spread(2, go, output)
    gather.finish()
    scatter = Scatter(
        place, w, (box_p, box_s, box_f, box_z), (send_p, send_s, send_f, send_z), (recv_p, recv_s, recv_f, recv_z),
        shard,
    )
    low_grad[...] = g2[...].astype(BF16)
    tall[0] = jnp.transpose(g2[...]).astype(BF16)
    tall[1] = jnp.transpose(hb[...].astype(F32)).astype(BF16)
    acc[...] = g2[...]

    def chunk(i, core):
        return ((place.y + 1 - i) % 2) * 2 + core

    def feed_back(t, store):
        grad_pre = dot(low_grad[...], w[2, t]) * gp[t].astype(F32)
        put_row(gsm, t, slice(0, 768), jnp.sum(grad_pre, axis=0, keepdims=True))
        gpre[...] = grad_pre.astype(BF16)
        store(2, dot(tall[0], act[t]))
        acc[...] += dot_nt(gpre[...], w[1, t])
        store(1, dot(tall[1], gpre[...]))

    @pl.loop(0, 2)
    def _(i):
        t = chunk(i, 1 - place.c)

        def store(k, value):
            w[k, t] = value.astype(BF16)
            scatter.to_partner(k, t, i)

        feed_back(t, store)

    @pl.loop(0, 2)
    def _(i):
        t = chunk(i, place.c)

        def store(k, value):
            scatter.from_partner(k, i)
            w[k, t] = (value + box_p[k, i].astype(F32)).astype(BF16)
            pl.when(i == 0)(lambda: scatter.ready(k, 0))
            pl.when(i == 1)(lambda: scatter.ready(k, 1))

        feed_back(t, store)

    @pl.loop(0, blocks)
    def _(r):
        rows = pl.ds(pl.multiple_of(r * ROWS, ROWS), ROWS)
        cot = acc[rows, :]
        normed = n1[rows, :]
        e = cot * sm[3:4, :]
        en = jnp.mean(e * normed, axis=1, keepdims=True)
        grad = s1[rows, 0:1] * (e - jnp.mean(e, axis=1, keepdims=True) - normed * en)
        acc[rows, :] = grad
        low_grad[rows, :] = grad.astype(BF16)
        gsm[2:3, :] += jnp.sum(grad, axis=0, keepdims=True)
        gsm[3:4, :] += jnp.sum(cot * normed, axis=0, keepdims=True)
        gsm[4:5, :] += jnp.sum(cot, axis=0, keepdims=True)

    tall[0] = jnp.transpose(acc[...]).astype(BF16)
    tall[1] = jnp.transpose(x[...].astype(F32)).astype(BF16)

    one_low, one_high = lane_masks(1.0)
    tall_bias = jnp.where(lax.broadcasted_iota(jnp.int32, (seq, 1), 0) < length, F32(0), F32(NEG))

    def attention_back(t, event, store):
        back = dot(low_grad[...], w[0, t, :, 512:768])
        gctx[:, 0:128] = pltpu.roll(jnp.where(is_low((seq, 128)), back[:, 0:128], 0.0), 64, 1).astype(BF16)
        gctx[:, 128:256] = back[:, 128:256].astype(BF16)
        log_rows = jnp.transpose(stat[t])
        grads_q = []
        grads_k = []
        grads_v = []
        for h in range(3):
            if h < 2:
                queries = qkv[t, :, 0:128] * (low, high)[h]
                keys = qkv[t, :, 128:256]
                values = qkv[t, :, 256:384]
                cots = gctx[:, 128:256] * (one_low, one_high)[h]
            else:
                queries = qkv[t, :, 640:768]
                keys = qkv[t, :, 384:512]
                values = qkv[t, :, 512:640]
                cots = gctx[:, 0:128]
            scores = dot_nt(keys, queries) + tall_bias
            probs = jnp.exp(scores - log_rows[h : h + 1, :])
            grad_probs = dot_nt(values, cots)
            row_dots = jnp.sum(grad_probs * probs, axis=0, keepdims=True)
            grad_scores = (probs * (grad_probs - row_dots)).astype(BF16)
            grads_v.append(dot(probs.astype(BF16), cots))
            grads_k.append(dot(grad_scores, queries))
            part = (0, HD, HD)[h]
            keys_tall = jnp.transpose(keys.astype(F32))[part : part + HD, :].astype(BF16)
            grads_q.append(dot(keys_tall, grad_scores) * 0.125)
        pair = jnp.transpose(jnp.concatenate([grads_q[0], grads_q[1]], axis=0))
        single = jnp.transpose(jnp.concatenate([grads_q[2], jnp.zeros_like(grads_q[2])], axis=0))
        tiles = [pair, grads_k[0] + grads_k[1], grads_v[0] + grads_v[1], single + grads_k[2], grads_v[2]]
        for i, tile in enumerate(tiles):
            span = slice(128 * i, 128 * i + 128)
            put_row(gsm, 4 + t, span, jnp.sum(tile, axis=0, keepdims=True))
            gpacked[:, span] = tile.astype(BF16)
        event()
        acc[...] += dot_nt(gpacked[...], w[0, t, :, 0:640])
        store(slice(0, 512), dot(tall[1], gpacked[:, 0:512]))
        store(slice(512, 640), dot(tall[1], gpacked[:, 512:640]) + dot(tall[0], ctx[t, :, 0:128]))
        store(slice(640, 768), dot(tall[0], ctx[t, :, 128:256]))

    @pl.loop(0, 2)
    def _(i):
        t = chunk(i, 1 - place.c)

        def store(span, value):
            w[0, t, :, span] = value.astype(BF16)

        def event():
            pl.when(i == 0)(lambda: scatter.add_far(2))
            pl.when(i == 1)(lambda: scatter.add_far(1))

        attention_back(t, event, store)
        scatter.to_partner(0, t, i)

    @pl.loop(0, 2)
    def _(i):
        t = chunk(i, place.c)

        def store(span, value):
            w[0, t, :, span] = (value + box_p[0, i, :, span].astype(F32)).astype(BF16)

        def event():
            pl.when(i == 0)(lambda: scatter.add_near(2))
            scatter.from_partner(0, i)

        attention_back(t, event, store)
        pl.when(i == 0)(lambda: scatter.ready(0, 0))
        pl.when(i == 1)(lambda: scatter.ready(0, 1))

    x[...] = acc[...].astype(BF16)
    stages[0] = gsm[...]
    sums = SmallSum(place, stages, small_box, small_send, small_recv)
    sums.start(0)
    scatter.add_near(1)
    scatter.add_far(0)
    tokens.spread(3, x, gtok)
    sums.step(0)
    scatter.add_last(2)
    sums.step(1)
    scatter.add_near(0)
    sums.step(2)
    scatter.add_last(1)
    sums.finish(small)
    scatter.add_last(0)
    for i in (2, 3):
        tokens.wait(i, x_in.at[0])
    scatter.finish()


def layer_call(dp_count, tokens, grad_out, own, small, length):
    part, width = tokens.shape[1], tokens.shape[2]
    seq = tokens.shape[0] * part
    shapes = (((4, part, width), BF16), ((4, part, width), BF16), ((3, 96, width), F32), ((16, width), F32))
    vmem = pl.BlockSpec(memory_space=pltpu.VMEM)
    smem = pl.BlockSpec(memory_space=pltpu.SMEM)
    dma = pltpu.SemaphoreType.DMA
    low_rows = pltpu.VMEM((seq, width), BF16)
    wide_rows = pltpu.VMEM((seq, width), F32)
    return pl.pallas_call(
        functools.partial(layer_kernel, dp_count),
        out_shape=[jax.ShapeDtypeStruct(s, d) for s, d in shapes],
        in_specs=[vmem] * 4 + [smem],
        out_specs=[vmem] * 4,
        scratch_shapes=[
            pltpu.VMEM((3, 4, width, 768), BF16), low_rows, low_rows, pltpu.VMEM((8, 16, width), BF16),
            pltpu.VMEM((16, width), F32), pltpu.VMEM((4, seq, 768), BF16), pltpu.VMEM((4, seq, 256), BF16),
            pltpu.VMEM((4, seq, 768), BF16), pltpu.VMEM((4, seq, 768), BF16), low_rows, wide_rows,
            pltpu.VMEM((seq, 128), F32), wide_rows, pltpu.VMEM((4, seq, 128), F32), pltpu.VMEM((16, width), F32),
            wide_rows, wide_rows, low_rows, pltpu.VMEM((2, width, seq), BF16), pltpu.VMEM((seq, 768), BF16),
            pltpu.VMEM((seq, 256), BF16), pltpu.VMEM((seq, 640), BF16),
            pltpu.VMEM((3, 2, width, 768), BF16), pltpu.VMEM((3, 2, 4, 96, width), BF16),
            pltpu.VMEM((3, 4, 96, width), BF16), pltpu.VMEM((3, 3, 96, width), BF16),
            pltpu.VMEM((4, 16, width), F32), pltpu.VMEM((6, 16, width), F32),
            dma((3, 31)), dma((3, 32)), dma((4, 4)), dma((4, 4)), dma((4,)), dma((4,)), dma((8,)), dma((8,)),
            dma((3, 2)), dma((3, 2)), dma((3, 8)), dma((3, 8)), dma((3, 4)), dma((3, 4)), dma((3, 3)), dma((3, 3)),
            dma((6,)), dma((6,)),
        ],
        compiler_params=pltpu.CompilerParams(
            vmem_limit_bytes=VMEM_LIMIT, collective_id=0, has_side_effects=True
        ),
        name="layer",
    )(tokens, grad_out, own, small, length)


def gather_groups(shard, dp_count, axis):
    stride = dp_count // 8
    if stride == 1:
        return shard
    groups = [[g * stride + i for i in range(stride)] for g in range(8)]
    return lax.all_gather(shard, "dp", axis=axis, tiled=True, axis_index_groups=groups)


def scatter_groups(shard, small, dp_count):
    stride = dp_count // 8
    if stride == 1:
        return shard, small
    groups = [[g * stride + i for i in range(stride)] for g in range(8)]
    shard = lax.psum_scatter(shard, "dp", scatter_dimension=1, tiled=True, axis_index_groups=groups)
    return shard, lax.psum(small, "dp", axis_index_groups=groups)


def pack_small(vectors, bias, dp_count, width):
    group = lax.axis_index("dp") // (dp_count // 8)
    part = vectors.shape[1]
    rows = lax.dynamic_update_slice(jnp.zeros((8, width), BF16), vectors, (0, group * part))
    units = lax.dynamic_update_slice(jnp.zeros((4 * width,), BF16), bias, (group * (4 * part),))
    qb = rows[0].reshape(4, 192)
    vb = rows[1].reshape(4, 192)
    none = jnp.zeros((4, 128), BF16)
    packed = jnp.concatenate([qb[:, :128], none, vb[:, :128], qb[:, 128:], none, vb[:, 128:], none], axis=1)
    return jnp.concatenate([rows, units.reshape(4, width), packed], axis=0)


def pack_attention(q, k, v, o):
    return jnp.concatenate(
        [q[:, :128], k[:, :128], v[:, :128], q[:, 128:], k[:, 128:], o[:, 128:], v[:, 128:], o[:, :128]], axis=1
    )


def shards(tokens, lengths, grad_out, qkv_weight, out_weight, up_weight, down_weight, vectors, hidden_bias):
    dp_count = lax.axis_size("dp")
    dp_rank = lax.axis_index("dp")
    tensor_rank = lax.axis_index("tensor")
    width = tokens.shape[2]
    part = width // dp_count

    own = jnp.stack([
        pack_attention(qkv_weight[0], qkv_weight[1], qkv_weight[2], out_weight.T), up_weight, down_weight.T
    ])
    own = gather_groups(own, dp_count, 1)
    small = pack_small(gather_groups(vectors, dp_count, 1), gather_groups(hidden_bias, dp_count, 0), dp_count, width)
    length = lax.dynamic_slice_in_dim(lengths, tensor_rank, 1).reshape(1, 1)
    output, gtok, g, gsm = layer_call(dp_count, tokens, grad_out, own, small, length)
    grad_tokens = gtok.astype(F32)
    g, gsm = scatter_groups(g, gsm, dp_count)
    a = g[0]
    gq = jnp.concatenate([a[:, 0:128], a[:, 384:448]], axis=1)
    gk = jnp.concatenate([a[:, 128:256], a[:, 448:512]], axis=1)
    gv = jnp.concatenate([a[:, 256:384], a[:, 576:640]], axis=1)
    gout = jnp.concatenate([a[:, 640:768], a[:, 512:576]], axis=1).T
    packed = gsm[12:16]
    row_q = jnp.concatenate([packed[:, 0:128], packed[:, 384:448]], axis=1).reshape(1, width)
    row_v = jnp.concatenate([packed[:, 256:384], packed[:, 576:640]], axis=1).reshape(1, width)
    rows = jnp.concatenate([row_q, row_v, gsm[2:8]], axis=0)
    grad_vectors = lax.dynamic_slice_in_dim(rows, dp_rank * part, part, 1)
    units = gsm[8:12].reshape(-1)
    grad_bias = lax.dynamic_slice_in_dim(units, dp_rank * (part * 4), part * 4)
    return output, grad_tokens, jnp.stack([gq, gk, gv]), gout, g[1], g[2].T, grad_vectors, grad_bias


def solution(mesh):
    in_specs = (
        P("dp", "tensor", None), P("dp"), P("dp", "tensor", None), P(None, "dp", "tensor"), P("tensor", "dp"),
        P("dp", "tensor"), P("tensor", "dp"), P(None, "dp"), P("dp"),
    )
    out_specs = (
        P("dp", "tensor", None), P("dp", "tensor", None), P(None, "dp", "tensor"), P("tensor", "dp"),
        P("dp", "tensor"), P("tensor", "dp"), P(None, "dp"), P("dp"),
    )
    return jax.shard_map(shards, mesh=mesh, in_specs=in_specs, out_specs=out_specs, check_vma=False)
```

time: 615 us -> 202 us (0.33)
  waiting for transfers between devices: 346 us -> 0 us
  blocking collectives: 115 us -> 0 us
  Pallas kernels: 90.9 us -> 183 us
  between operations: 14.1 us -> 0.78 us
  starting transfers between devices: 11.6 us -> 0 us
  other arithmetic: 15.8 us -> 5.13 us
  local copies, waits for them, and re-layouts: 20.9 us -> 12.6 us
    unnamed x5 -> x0, waiting for transfers between devices: 244 us -> none
    all_gather x2 -> x0, waiting for transfers between devices: 93.8 us -> none  [the longest x1 67.4 us: shards(): lax.all_gather(own, 'dp', axis=1, tiled=True)]
    pallas_call x2 -> x1, Pallas kernels: 90.9 us -> 183 us  [layer_call(): pl.pallas_call(functools.partial(layer_kernel, dp_count), out_shape=[jax....]
    all_gather x2 -> x0, blocking collectives: 52.1 us -> none  [the longest x1 26.1 us: shards(): vec = lax.all_gather(vectors, 'dp', axis=1, tiled=True).astype(F32)]
    psum x1 -> x0, blocking collectives: 46.3 us -> none  [shards(): gsm = lax.psum(gsm, ('dp', 'tensor'))]
    all_to_all x1 -> x0, blocking collectives: 16.5 us -> none  [shards(): x = lax.all_to_all(tokens, 'tensor', 0, 1, tiled=True)[0]]
    all_to_all x3 -> x0, starting transfers between devices: 11.2 us -> none  [the longest x1 4.2 us: shards(): go = lax.all_to_all(grad_out, 'tensor', 0, 1, tiled=True)[0]]
    unnamed x2 -> x0, other arithmetic: 10.9 us -> none
  transfers between devices with their start and end apart: 7 -> 0, of which waited for: 4 -> 0; matrix products, arithmetic and copies ran while one was open for 4% -> 0% of each run, Pallas kernels for 0% -> 0%
where the time goes in v3:
time: 202 us
  Pallas kernels  183 us (91%)
  local copies, waits for them, and re-layouts  12.6 us (6%)
  other arithmetic  5.13 us (3%)
    pallas_call x1, Pallas kernels, layer_call(): pl.pallas_call(functools.partial(layer_kernel, dp_count), out_shape=[jax....  183 us

profile of v3, /device:TPU:0, one launch (start us, length us, event | category | flops | bytes accessed | tf_op | source)
XLA Modules:
  0.0 201.8 jit_solution(9290429288933580061)
XLA Ops:
  0.6 1.2 dynamic_slice.9
  1.9 0.9 dynamic_update_slice.7
  2.8 0.8 dynamic_update_slice.6
  3.6 0.1 reshape_squeeze.7
  3.7 0.1 reshape_squeeze.6
  3.8 0.1 concatenate.31
  3.9 0.6 pad_maximum_fusion.2.small_in
  4.5 0.9 copy.17
  5.4 0.9 slice_bitcast_fusion.3
  6.4 0.1 concatenate.30
  6.5 1.8 pad_maximum_fusion.own
  8.3 183.2 %layer.1 = (bf16[4,128,768]{2,1,0:T(8,128)(2,1)}, bf16[4,128,768]{2,1,0:T(8,128)(2,1)}, f32[3,96,768]{2,1,0:T(8,128)}, f32[16,768]{1,0:T(8,128)}) custom-call(bf16[4,128,768]{2,1,0:T(8,128)(2,1)} %x_in.1, bf16[4,128,768]{2,1,0:T(8,128)(2,1)} %go_in.1, bf16[3,96,768]{2,1,0:T(8,128)(2,1)} %pad_maximum_fusion.own, bf16[16,768]{1,0:T(8,128)(2,1)} %pad_maximum_fusion.2.small_in, ...), custom_call_target="tpu_custom_call" | custom-call | tf_op jit(solution)/shard_map/layer/pallas_call | solution.py:648
  191.5 0.8 fusion.5
  192.3 0.7 fusion.4
  193.0 0.1 reshape.33
  193.1 0.1 reshape.34
  193.1 0.7 slice.140
  193.9 0.7 slice.139
  194.6 0.7 fusion.1
  195.3 0.7 dynamic_slice.11
  196.0 2.0 slice_bitcast_fusion
  198.0 0.0 copy-start.1
  198.0 0.1 fusion.3
  198.1 0.7 copy.18
  198.9 0.0 copy-start
  198.9 0.7 pad_maximum_fusion.1
  199.6 0.0 copy-done.1
  199.6 1.3 convert_element_type.3
  200.9 0.0 copy-done
  200.9 0.9 copy.22
  (23 shorter events, 0.2 us)
Async XLA Ops:
  198.0 1.7 copy-start.1
  198.9 2.0 %copy-start = (bf16[4,128,768]{2,1,0:T(8,128)(2,1)S(1)}, bf16[4,128,768]{2,1,0:T(8,128)(2,1)}, u32[]{:S(2)}) copy-start(bf16[4,128,768]{2,1,0:T(8,128)(2,1)} %get-tuple-element.56) | copy-start | bytes 2359300

commit v4 on v3

--- a/solution.py
+++ b/solution.py
@@ -55,18 +55,16 @@
     def device(self, z, x, y, c):
         return ((z * 2 + x) * self.stride + self.rest, y * 2 + c)
 
-    def shifted(self, j, second, first, other=False):
-        if other:
-            second, first = first, second
-        across_x = self.c * second + (1 - self.c) * first
-        across_y = self.c * first + (1 - self.c) * second
+    def shifted(self, j, second, first, swapped):
+        across_x = swapped * second + (1 - swapped) * first
+        across_y = swapped * first + (1 - swapped) * second
         return (self.z + j) % 4, (self.x + across_x) % 2, (self.y + across_y) % 2
 
-    def first(self):
-        return self.device(*self.shifted(0, 0, 1), self.c)
-
-    def second(self):
-        return self.device(*self.shifted(0, 1, 0), self.c)
+    def first(self, swapped):
+        return self.device(*self.shifted(0, 0, 1, swapped), self.c)
+
+    def second(self, swapped):
+        return self.device(*self.shifted(0, 1, 0, swapped), self.c)
 
     def partner(self):
         return self.device(self.z, self.x, self.y, 1 - self.c)
@@ -102,37 +100,43 @@
         self.place, self.own, self.w, self.send, self.recv = place, own, w, send, recv
 
     def piece(self, k, s, f, j):
-        z, x, y = self.place.shifted(j, s, f)
+        z, x, y = self.place.shifted(j, s, f, self.swapped(k))
         return self.w.at[k, y * 2 + self.place.c, pl.ds(pl.multiple_of((z * 2 + x) * 96, 96), 96), :]
+
+    def swapped(self, k):
+        return 1 if k == 1 else self.place.c
 
     def push(self, k, src, dst, send, recv, device):
         remote(src, dst, self.send.at[k, send], self.recv.at[k, recv], device).start()
 
     def forward(self, k, s, f, j, to):
         here = self.piece(k, s, f, j)
-        src = self.own.at[k] if (s, f, j) == (0, 0, 0) else here
+        src = self.own[k] if (s, f, j) == (0, 0, 0) else here
         if "f" in to:
-            self.push(k, src, here, 3 + j, 4 + j, self.place.first())
+            self.push(k, src, here, 3 + j, 4 + j, self.place.first(self.swapped(k)))
         if "s" in to:
-            self.push(k, src, here, 7 + 4 * f + j, 8 + 4 * f + j, self.place.second())
+            self.push(k, src, here, 7 + 4 * f + j, 8 + 4 * f + j, self.place.second(self.swapped(k)))
         if "p" in to:
             self.push(k, src, here, 15 + 8 * s + 4 * f + j, 16 + 8 * s + 4 * f + j, self.place.partner())
 
-    def along(self, k):
+    def along(self, k, f=0):
+        here = self.piece(k, 0, f, 0)
         for j in (1, 3, 2):
-            self.push(k, self.own.at[k], self.piece(k, 0, 0, 0), j - 1, 4 - j, self.place.along(j))
+            self.push(k, here if f else self.own[k], here, 4 * f + j - 1, 4 * f + 4 - j, self.place.along(j))
 
     def start(self, k):
         self.forward(k, 0, 0, 0, "fsp")
 
     def wait(self, k, slot):
-        here = self.own.at[k]
+        here = self.own[k]
         remote(here, here, self.send.at[k, 0], self.recv.at[k, slot], self.place.partner()).wait_recv()
 
     def relay(self, k, s, f, order):
         for j in order:
             self.wait(k, 8 * s + 4 * f + j)
-            self.forward(k, s, f, j, "p" if s else "sp" if f else "fsp")
+            if k == 2 and (s, f, j) == (0, 1, 0):
+                self.along(k, 1)
+            self.forward(k, s, f, j, "p" if s else "sp" if f or k == 2 else "fsp")
 
     def others(self, k):
         @pl.loop(16, 32)
@@ -141,7 +145,7 @@
 
     def finish(self):
         for k in range(3):
-            here = self.own.at[k]
+            here = self.own[k]
 
             @pl.loop(0, 31)
             def _(slot):
@@ -152,90 +156,119 @@
     def __init__(self, place, g, boxes, sends, recvs, out):
         self.place, self.g, self.boxes, self.sends, self.recvs, self.out = place, g, boxes, sends, recvs, out
 
-    def push(self, stage, src, index, sem, device):
+    def box(self, stage, part, *index):
+        return self.boxes[stage].at[(part[1], *index, slice(None), pl.ds(*part[2]))]
+
+    def push(self, stage, part, f_from, s_from, j, index, sem, device):
+        k, t, row = self.piece(part, s_from, f_from, j)
+        src = self.g.at[k, t, pl.ds(row, 96), pl.ds(*part[2])]
         remote(
-            src, self.boxes[stage].at[index], self.sends[stage].at[sem], self.recvs[stage].at[sem], device
+            src, self.box(stage, part, *index), self.sends[stage].at[part[0], sem],
+            self.recvs[stage].at[part[0], sem], device,
         ).start()
 
-    def piece(self, k, s, f, j):
-        z, x, y = self.place.shifted(j, s, f)
-        return k, y * 2 + self.place.c, pl.multiple_of((z * 2 + x) * 96, 96)
-
-    def view(self, k, s, f, j):
-        kind, t, row = self.piece(k, s, f, j)
-        return self.g.at[kind, t, pl.ds(row, 96), :]
-
-    def wait(self, stage, index, sem):
-        here = self.boxes[stage].at[index]
-        remote(here, here, self.sends[stage].at[sem], self.recvs[stage].at[sem], self.place.partner()).wait_recv()
+    def piece(self, part, s, f, j):
+        z, x, y = self.place.shifted(j, s, f, self.place.c)
+        return part[1], y * 2 + self.place.c, pl.multiple_of((z * 2 + x) * 96, 96)
+
+    def wait(self, stage, part, index, sem):
+        here = self.box(stage, part, *index)
+        remote(
+            here, here, self.sends[stage].at[part[0], sem], self.recvs[stage].at[part[0], sem], self.place.partner()
+        ).wait_recv()
+
+    def chunk_copy(self, k, t, i):
+        return remote(
+            self.g.at[k, t], self.boxes[0].at[k, i], self.sends[0].at[k, i], self.recvs[0].at[k, i],
+            self.place.partner(),
+        )
 
     def to_partner(self, k, t, i):
-        self.push(0, self.g.at[k, t], (k, i), (k, i), self.place.partner())
+        self.chunk_copy(k, t, i).start()
 
     def from_partner(self, k, i):
-        self.wait(0, (k, i), (k, i))
-
-    def across(self, k, f):
+        self.chunk_copy(k, 0, i).wait_recv()
+
+    def across(self, part, f):
         for j in (2, 1, 3, 0):
-            self.push(1, self.view(k, 1, f, j), (k, f, j), (k, 4 * f + j), self.place.second())
-
-    def ready(self, k, i):
+            self.push(1, part, f, 1, j, (f, j), 4 * f + j, self.place.second(self.place.c))
+
+    def ready(self, parts, i):
         if i == 0:
-            self.across(k, 1)
-
-            @pl.when(self.place.c == 0)
-            def _():
-                self.across(k, 0)
-        else:
-            @pl.when(self.place.c == 1)
-            def _():
-                self.across(k, 0)
-
-    def total(self, k, f, j, parts, last=False):
-        kind, t, row = self.piece(k, 0, f, j)
+            for part in parts:
+                self.across(part, 1)
+
+        @pl.when(self.place.c == i)
+        def _():
+            for part in parts:
+                self.across(part, 0)
+
+    def total(self, part, f, j, views, last=False):
+        k, t, row = self.piece(part, 0, f, j)
+        columns = pl.ds(*part[2])
 
         @pl.loop(0, 3)
         def _(r):
             lines = pl.ds(pl.multiple_of(row + r * 32, 32), 32)
             local = pl.ds(pl.multiple_of(r * 32, 32), 32)
-            value = self.g[kind, t, lines, :].astype(F32)
-            for stage, index in parts:
-                value += self.boxes[stage][(*index, local, slice(None))].astype(F32)
+            value = self.g[k, t, lines, columns].astype(F32)
+            for stage, index in views:
+                value += self.boxes[stage][(k, *index, local, columns)].astype(F32)
             if last:
-                self.out[k, local, :] = value
+                self.out[k, local, columns] = value
             else:
-                self.g[kind, t, lines, :] = value.astype(BF16)
-
-    def add_far(self, k):
+                self.g[k, t, lines, columns] = value.astype(BF16)
+
+    def add(self, part, f, j, arrived, last=False):
+        for stage, index, sem in arrived:
+            self.wait(stage, part, index, sem)
+        self.total(part, f, j, [(stage, index) for stage, index, _ in arrived], last)
+
+    def add_far(self, part):
         for j in (2, 1, 3, 0):
-            self.wait(1, (k, 1, j), (k, 4 + j))
-            self.total(k, 1, j, [(1, (k, 1, j))])
-            self.push(2, self.view(k, 0, 1, j), (k, j), (k, j), self.place.first())
-
-    def add_near(self, k):
+            self.add(part, 1, j, [(1, (1, j), 4 + j)])
+            self.push(2, part, 1, 0, j, (j,), j, self.place.first(self.place.c))
+
+    def add_near(self, part):
         for j in (2, 1, 3):
-            self.wait(1, (k, 0, j), (k, j))
-            self.wait(2, (k, j), (k, j))
-            self.total(k, 0, j, [(1, (k, 0, j)), (2, (k, j))])
-            self.push(3, self.view(k, 0, 0, j), (k, 3 - j), (k, 3 - j), self.place.along(j))
-
-    def add_last(self, k):
-        self.wait(1, (k, 0, 0), (k, 0))
-        self.wait(2, (k, 0), (k, 0))
-        for i in range(3):
-            self.wait(3, (k, i), (k, i))
-        self.total(k, 0, 0, [(1, (k, 0, 0)), (2, (k, 0)), (3, (k, 0)), (3, (k, 1)), (3, (k, 2))], True)
-
-    def finish(self):
-        counts = ((0, 2), (1, 8), (2, 4), (3, 3))
+            self.add(part, 0, j, [(1, (0, j), j), (2, (j,), j)])
+            self.push(3, part, 0, 0, j, (3 - j,), 3 - j, self.place.along(j))
+
+    def add_last(self, part):
+        arrived = [(1, (0, 0), 0), (2, (0,), 0), (3, (0,), 0), (3, (1,), 1), (3, (2,), 2)]
+        self.add(part, 0, 0, arrived, True)
+
+    def line_far(self, part):
+        for j in (2, 1, 3):
+            self.add(part, 1, j, [(1, (1, j), 4 + j)])
+            self.push(2, part, 1, 0, j, (3 - j,), 3 - j, self.place.along(j))
+
+    def line_near(self, part):
+        for j in (2, 1, 3):
+            self.add(part, 0, j, [(1, (0, j), j)])
+            self.push(3, part, 0, 0, j, (3 - j,), 3 - j, self.place.along(j))
+
+    def line_turn(self, part):
+        self.add(part, 1, 0, [(1, (1, 0), 4), (2, (0,), 0), (2, (1,), 1), (2, (2,), 2)])
+        self.push(2, part, 1, 0, 0, (3,), 3, self.place.first(self.place.c))
+
+    def line_last(self, part):
+        arrived = [(1, (0, 0), 0), (3, (0,), 0), (3, (1,), 1), (3, (2,), 2), (2, (3,), 3)]
+        self.add(part, 0, 0, arrived, True)
+
+    def finish(self, parts):
         for k in range(3):
-            for stage, count in counts:
-                here = self.g.at[0, 0] if stage == 0 else self.boxes[2].at[0, 0]
+            for i in range(2):
+                self.chunk_copy(k, 0, i).wait_send()
+        for part in parts:
+            for stage, count in ((1, 8), (2, 4), (3, 3)):
+                here = self.box(2, part, 0)
 
                 @pl.loop(0, count)
                 def _(i):
                     remote(
-                        here, here, self.sends[stage].at[k, i], self.recvs[stage].at[k, i], self.place.partner()
+                        here, here, self.sends[stage].at[part[0], i], self.recvs[stage].at[part[0], i],
+                        self.place.partner(),
                     ).wait_send()
 
 
@@ -250,8 +283,9 @@
         self.sent.append(copy)
 
     def start(self, i):
+        peers = (self.place.partner(), self.place.second(self.place.c), self.place.first(self.place.c))
         if i < 3:
-            self.push(i, i, (self.place.partner, self.place.second, self.place.first)[i]())
+            self.push(i, i, peers[i])
         else:
             for j in range(1, 4):
                 self.push(3, 6 - j, self.place.along(j))
@@ -308,11 +342,126 @@
             pltpu.make_async_copy(block, block, self.local.at[i]).wait()
 
 
+def steps(k, s, f, *order):
+    return k, s, f, order
+
+
+EARLY = (
+    steps(0, 0, 1, 0), steps(0, 0, 0, 1, 3), steps(1, 0, 1, 0), steps(2, 0, 1, 0), steps(0, 0, 0, 2),
+    steps(0, 0, 1, 1, 3), steps(0, 1, 0, 0), steps(0, 1, 1, 0), steps(0, 0, 1, 2), steps(1, 0, 0, 1),
+    steps(0, 1, 0, 1, 3), steps(0, 1, 1, 1, 3), steps(1, 0, 0, 3), steps(0, 1, 0, 2), steps(0, 1, 1, 2),
+)
+X_AFTER = 6
+IN_ATTENTION = (
+    (steps(1, 0, 0, 2),), (steps(1, 0, 1, 1, 3),), (steps(1, 1, 0, 0),), (steps(1, 1, 1, 0), steps(2, 1, 0, 0)),
+    (steps(2, 0, 0, 1),), (steps(1, 0, 1, 2),), (steps(1, 1, 0, 1, 3), steps(2, 1, 1, 0)), (steps(1, 1, 1, 1),),
+    (steps(1, 1, 1, 3), steps(2, 0, 0, 3)), (steps(1, 1, 0, 2),), (steps(2, 0, 0, 2),), (steps(1, 1, 1, 2),),
+)
+IN_UP = (
+    (steps(2, 0, 1, 1),), (steps(2, 1, 0, 1),), (steps(2, 1, 0, 3),), (steps(2, 0, 1, 3),), (steps(2, 1, 0, 2),),
+    (steps(2, 1, 1, 1),), (steps(2, 0, 1, 2),), (steps(2, 1, 1, 3),),
+)
+LATE = (steps(2, 1, 1, 2),)
+DOWN, UP, FRONT, BACK = (2, 2, (0, 768)), (1, 1, (0, 768)), (0, 0, (0, 512)), (3, 0, (512, 256))
+
+
+def spots(rows, offset, gap=0):
+    source = lax.broadcasted_iota(jnp.int32, (96, 768), 0) + rows
+    target = lax.broadcasted_iota(jnp.int32, (96, 768), 1)
+    moved = source + offset + jnp.where(source < 128, 0, gap)
+    return jnp.where(target == moved, F32(1), F32(0)).astype(BF16)
+
+
+def pack_small(place, vec_in, bias_in):
+    group = place.z * 2 + place.x
+    rows = vec_in[...]
+    top = dot(rows, spots(96 * group, 0, 0))
+    start = 96 * (group % 2)
+    queries = dot(rows, spots(start, 0, 256))[0:1]
+    values = dot(rows, spots(start, 256, 192))[1:2]
+    units = bias_in[...].astype(F32)
+    lane = lax.broadcasted_iota(jnp.int32, (1, 768), 1)
+    units = jnp.where(lane // 384 == group % 2, jnp.concatenate([units, units], axis=1), 0.0)
+    line = lax.broadcasted_iota(jnp.int32, (8, 768), 0)
+    low = jnp.where(line == group // 2, units, 0.0) + jnp.where(line == 4 + group // 2, queries + values, 0.0)
+    return jnp.concatenate([top, low], axis=0).astype(BF16)
+
+
+def pack_attention(qkv_in, out_in):
+    q, k, v = (qkv_in[i].astype(F32) for i in range(3))
+    o = jnp.transpose(out_in[...].astype(F32))
+    return jnp.concatenate([
+        q[:, :128], k[:, :128], v[:, :128], jnp.concatenate([q[:, 128:], k[:, 128:]], axis=1),
+        jnp.concatenate([o[:, 128:], v[:, 128:]], axis=1), o[:, :128],
+    ], axis=1).astype(BF16)
+
+
+def finish_kernel(
+    dp_count, out_in, gtok_in, shard, small,
+    output, gtok, qkv, out, up, down, vec, units,
+):
+    stride = dp_count // 8
+    rank = lax.axis_index("dp")
+    group, part = rank // stride, vec.shape[1]
+    output[...] = out_in[...]
+    gtok[...] = gtok_in[...].astype(F32)
+    a = shard[0]
+    qkv[0, :, 0:128] = a[:, 0:128]
+    qkv[1, :, 0:128] = a[:, 128:256]
+    qkv[2, :, 0:128] = a[:, 256:384]
+    qkv[0, :, 128:192] = a[:, 384:448]
+    qkv[1, :, 128:192] = pltpu.roll(a[:, 384:512], 64, 1)[:, 0:64]
+    qkv[2, :, 128:192] = pltpu.roll(a[:, 512:640], 64, 1)[:, 0:64]
+    out[0:128, :] = jnp.transpose(a[:, 640:768])
+    out[128:192, :] = jnp.transpose(a[:, 512:640])[0:64]
+    up[...] = shard[1]
+    down[...] = shard[2]
+
+    rest = rank % stride
+    even = group % 2 == 0
+    lane = lax.broadcasted_iota(jnp.int32, (1, 768), 1)
+
+    def own_lines(row, first, second):
+        near = pltpu.roll(row, jnp.where(even, (768 - first) % 768, 768 - first - 96), 1)
+        far = pltpu.roll(row, 768 - second + 32, 1)
+        return jnp.where(even | (lane < 32), near, far)
+
+    line = lax.broadcasted_iota(jnp.int32, (8, 768), 0)
+    packed = small[8:16, :]
+    row = jnp.sum(jnp.where(line == 4 + group // 2, packed, 0.0), axis=0, keepdims=True)
+    queries = own_lines(row, 0, 384)
+    values = own_lines(row, 256, 576)
+    lines = pltpu.roll(small[0:8, :], (768 - 96 * group) % 768, 1)
+    lines = jnp.where(line == 0, queries, jnp.where(line == 1, values, lines))
+    lines = pltpu.roll(lines, (768 - rest * part) % 768, 1)
+    vec[...] = lines[:, 0:part]
+    row = jnp.sum(jnp.where(line == group // 2, packed, 0.0), axis=0, keepdims=True)
+    shift = 384 * (group % 2) + rest * 4 * part
+    units[...] = pltpu.roll(row, (768 - shift) % 768, 1)[:, 0 : 4 * part]
+
+
+def finish_call(dp_count, out, gtok, shard, small):
+    rows, width = shard.shape[1], shard.shape[2]
+    shapes = (
+        (out.shape, BF16), (gtok.shape, F32), ((3, rows, width // 4), F32), ((width // 4, rows), F32),
+        ((rows, width), F32), ((rows, width), F32), ((8, rows), F32), ((1, 4 * rows), F32),
+    )
+    vmem = pl.BlockSpec(memory_space=pltpu.VMEM)
+    return pl.pallas_call(
+        functools.partial(finish_kernel, dp_count),
+        out_shape=[jax.ShapeDtypeStruct(s, d) for s, d in shapes],
+        in_specs=[vmem] * 4,
+        out_specs=[vmem] * 8,
+        compiler_params=pltpu.CompilerParams(vmem_limit_bytes=32 * 1024 * 1024),
+        name="finish",
+    )(out, gtok, shard, small)
+
+
 def layer_kernel(
-    dp_count, x_in, go_in, own, small_in, len_ref,
+    dp_count, x_in, go_in, qkv_in, out_in, up_in, down_in, vec_in, bias_in, len_ref,
     output, gtok, shard, small,
-    w, x, go, smalls, sm, qkv, ctx, act, gp, hb, n1, s1, g2, stat, gsm,
-    acc, pre, low_grad, tall, gpre, gctx, gpacked,
+    own_first, small_in, w, x, go, smalls, sm, qkv, ctx, act, gp, hb, n1, s1, stat, gsm,
+    acc, pre, low_grad, tall, gctx, gpacked,
     box_p, box_s, box_f, box_z, stages, small_box,
     send, recv, tok_send, tok_recv, tok_local, own_local, bias_send, bias_recv,
     send_p, recv_p, send_s, recv_s, send_f, recv_f, send_z, recv_z, small_send, small_recv,
@@ -320,17 +469,17 @@
     seq, width = x.shape
     blocks = seq // ROWS
     place = Place(dp_count)
+    own = (own_first, up_in, down_in)
     gather = Gather(place, own, w, send, recv)
+    own_first[...] = pack_attention(qkv_in, out_in)
+    small_in[...] = pack_small(place, vec_in, bias_in)
     tokens = Tokens(place, tok_send, tok_recv, tok_local)
-    near = (0, 1, 3, 2)
-    line = (1, 3, 2)
 
     barrier(place)
     gather.along(0)
     gather.start(0)
-    tokens.gather(0, x_in, x)
     for k in range(3):
-        pltpu.make_async_copy(own.at[k], gather.piece(k, 0, 0, 0), own_local.at[k]).start()
+        pltpu.make_async_copy(own[k], gather.piece(k, 0, 0, 0), own_local.at[k]).start()
     pltpu.make_async_copy(small_in, smalls.at[0], own_local.at[3]).start()
     for j in range(4):
         for i in range(2):
@@ -339,17 +488,16 @@
                 remote(
                     small_in, smalls.at[slot], bias_send.at[slot], bias_recv.at[slot], place.in_dp(j, i)
                 ).start()
-    gather.along(1)
-    gather.start(1)
-    gather.along(2)
-    gather.relay(0, 0, 0, line)
-    gather.relay(0, 0, 1, near)
-    gather.relay(0, 1, 0, near)
-    gather.relay(1, 0, 0, line)
-    gather.relay(0, 1, 1, near)
-    gather.start(2)
+    for k in (1, 2):
+        gather.along(k)
+        gather.start(k)
+    for event in EARLY[:X_AFTER]:
+        gather.relay(*event)
+    tokens.gather(0, x_in, x)
+    for event in EARLY[X_AFTER:]:
+        gather.relay(*event)
     for k in range(3):
-        pltpu.make_async_copy(own.at[k], own.at[k], own_local.at[k]).wait()
+        pltpu.make_async_copy(own[k], own[k], own_local.at[k]).wait()
     pltpu.make_async_copy(small_in, small_in, own_local.at[3]).wait()
 
     @pl.loop(1, 8)
@@ -364,23 +512,21 @@
     gather.others(0)
 
     low, high = lane_masks(0.125)
-    length = len_ref[0, 0]
+    length = len_ref[place.y * 2 + place.c]
     key_bias = jnp.where(lax.broadcasted_iota(jnp.int32, (1, seq), 1) < length, F32(0), F32(NEG))
     acc[...] = jnp.zeros_like(acc)
 
-    attention_events = {
-        0: lambda: gather.relay(1, 0, 1, (0, 1)),
-        1: lambda: gather.relay(1, 0, 1, (3, 2)),
-        2: lambda: gather.relay(2, 0, 0, line),
-        3: lambda: gather.relay(1, 1, 0, near),
-        4: lambda: tokens.gather(1, go_in, go),
-        5: lambda: gather.relay(1, 1, 1, near),
-        6: lambda: gather.relay(2, 0, 1, (0, 1)),
-        7: lambda: gather.relay(2, 0, 1, (3, 2)),
-    }
+    def relays(step, table):
+        for n, events in enumerate(table):
+            if events:
+                @pl.when(step == n)
+                def _():
+                    for event in events:
+                        gather.relay(*event)
 
     @pl.loop(0, 4)
     def _(t):
+        relays(3 * t, IN_ATTENTION)
         proj = dot(x[...], w[0, t, :, 0:640]) + sm[pl.ds(12 + t, 1), 0:640]
         qkv[t, :, 0:640] = proj.astype(BF16)
         q_two = pltpu.roll(jnp.where(is_low((seq, 128)), proj[:, 384:512] * 0.125, 0.0), 64, 1)
@@ -388,8 +534,7 @@
 
         @pl.loop(0, seq // 256)
         def _(r):
-            for slot, event in attention_events.items():
-                pl.when(t * 2 + r == slot)(event)
+            relays(3 * t + r + 1, IN_ATTENTION)
             rows = pl.ds(pl.multiple_of(r * 256, 256), 256)
             q_pair = qkv[t, rows, 0:128]
             outs = []
@@ -431,19 +576,14 @@
         hb[rows, :] = hidden.astype(BF16)
         acc[rows, :] = hidden + sm[5:6, :]
 
-    gather.relay(2, 1, 0, (0, 1))
     gather.others(1)
-    up_events = {
-        1: lambda: gather.relay(2, 1, 0, (3, 2)),
-        2: lambda: gather.relay(2, 1, 1, (0, 1)),
-        3: lambda: gather.relay(2, 1, 1, (3, 2)),
-    }
 
     @pl.loop(0, 4)
     def _(t):
-        for slot, event in up_events.items():
-            pl.when(t == slot)(event)
+        relays(2 * t, IN_UP)
         pre[...] = dot(hb[...], w[1, t])
+
+        relays(2 * t + 1, IN_UP)
 
         @pl.loop(0, blocks)
         def _(r):
@@ -454,13 +594,15 @@
             act[t, rows, :] = (u * cdf).astype(BF16)
             gp[t, rows, :] = (cdf + u * density).astype(BF16)
 
+    for event in LATE:
+        gather.relay(*event)
+    tokens.gather(1, go_in, go)
     gather.others(2)
 
     @pl.loop(0, 4)
     def _(t):
         acc[...] += dot_nt(act[t], w[2, t])
 
-    tokens.wait(1, x_in.at[0])
     gsm[...] = jnp.zeros_like(gsm)
 
     @pl.loop(0, blocks)
@@ -469,14 +611,24 @@
         resid = acc[rows, :]
         centred = resid - jnp.mean(resid, axis=1, keepdims=True)
         scale = lax.rsqrt(jnp.mean(centred * centred, axis=1, keepdims=True) + EPS)
-        normed = centred * scale
+        acc[rows, :] = centred * scale
+        pre[rows, 0:128] = jnp.broadcast_to(scale, (ROWS, 128))
+
+    tall[1] = jnp.transpose(hb[...].astype(F32)).astype(BF16)
+    tokens.wait(1, x_in.at[0])
+
+    @pl.loop(0, blocks)
+    def _(r):
+        rows = pl.ds(pl.multiple_of(r * ROWS, ROWS), ROWS)
+        normed = acc[rows, :]
         gain = sm[6:7, :]
         cot = go[rows, :].astype(F32)
         go[rows, :] = (normed * gain + sm[7:8, :]).astype(BF16)
         e = cot * gain
         en = jnp.mean(e * normed, axis=1, keepdims=True)
-        grad = scale * (e - jnp.mean(e, axis=1, keepdims=True) - normed * en)
-        g2[rows, :] = grad
+        grad = pre[rows, 0:1] * (e - jnp.mean(e, axis=1, keepdims=True) - normed * en)
+        acc[rows, :] = grad
+        low_grad[rows, :] = grad.astype(BF16)
         gsm[5:6, :] += jnp.sum(grad, axis=0, keepdims=True)
         gsm[6:7, :] += jnp.sum(cot * normed, axis=0, keepdims=True)
         gsm[7:8, :] += jnp.sum(cot, axis=0, keepdims=True)
@@ -487,43 +639,39 @@
         place, w, (box_p, box_s, box_f, box_z), (send_p, send_s, send_f, send_z), (recv_p, recv_s, recv_f, recv_z),
         shard,
     )
-    low_grad[...] = g2[...].astype(BF16)
-    tall[0] = jnp.transpose(g2[...]).astype(BF16)
-    tall[1] = jnp.transpose(hb[...].astype(F32)).astype(BF16)
-    acc[...] = g2[...]
+    tall[0] = jnp.transpose(acc[...]).astype(BF16)
 
     def chunk(i, core):
         return ((place.y + 1 - i) % 2) * 2 + core
 
-    def feed_back(t, store):
+    def own_chunk(k, i, t, value):
+        scatter.from_partner(k, i)
+        w[k, t] = (value + box_p[k, i].astype(F32)).astype(BF16)
+        parts = (DOWN,) if k == 2 else (UP,)
+        pl.when(i == 0)(lambda: scatter.ready(parts, 0))
+        pl.when(i == 1)(lambda: scatter.ready(parts, 1))
+
+    def down_back(t):
         grad_pre = dot(low_grad[...], w[2, t]) * gp[t].astype(F32)
         put_row(gsm, t, slice(0, 768), jnp.sum(grad_pre, axis=0, keepdims=True))
-        gpre[...] = grad_pre.astype(BF16)
-        store(2, dot(tall[0], act[t]))
-        acc[...] += dot_nt(gpre[...], w[1, t])
-        store(1, dot(tall[1], gpre[...]))
-
-    @pl.loop(0, 2)
-    def _(i):
-        t = chunk(i, 1 - place.c)
-
-        def store(k, value):
-            w[k, t] = value.astype(BF16)
+        gp[t] = grad_pre.astype(BF16)
+        return dot(tall[0], act[t])
+
+    def up_back(t):
+        acc[...] += dot_nt(gp[t], w[1, t])
+        return dot(tall[1], gp[t])
+
+    for k, back in ((2, down_back), (1, up_back)):
+        @pl.loop(0, 2)
+        def _(i):
+            t = chunk(i, 1 - place.c)
+            w[k, t] = back(t).astype(BF16)
             scatter.to_partner(k, t, i)
 
-        feed_back(t, store)
-
-    @pl.loop(0, 2)
-    def _(i):
-        t = chunk(i, place.c)
-
-        def store(k, value):
-            scatter.from_partner(k, i)
-            w[k, t] = (value + box_p[k, i].astype(F32)).astype(BF16)
-            pl.when(i == 0)(lambda: scatter.ready(k, 0))
-            pl.when(i == 1)(lambda: scatter.ready(k, 1))
-
-        feed_back(t, store)
+        @pl.loop(0, 2)
+        def _(i):
+            t = chunk(i, place.c)
+            own_chunk(k, i, t, back(t))
 
     @pl.loop(0, blocks)
     def _(r):
@@ -595,8 +743,8 @@
             w[0, t, :, span] = value.astype(BF16)
 
         def event():
-            pl.when(i == 0)(lambda: scatter.add_far(2))
-            pl.when(i == 1)(lambda: scatter.add_far(1))
+            pl.when(i == 0)(lambda: scatter.line_far(DOWN))
+            pl.when(i == 1)(lambda: scatter.line_near(DOWN))
 
         attention_back(t, event, store)
         scatter.to_partner(0, t, i)
@@ -609,34 +757,38 @@
             w[0, t, :, span] = (value + box_p[0, i, :, span].astype(F32)).astype(BF16)
 
         def event():
-            pl.when(i == 0)(lambda: scatter.add_near(2))
+            pl.when(i == 0)(lambda: scatter.add_far(UP))
+            pl.when(i == 1)(lambda: scatter.line_turn(DOWN))
             scatter.from_partner(0, i)
 
         attention_back(t, event, store)
-        pl.when(i == 0)(lambda: scatter.ready(0, 0))
-        pl.when(i == 1)(lambda: scatter.ready(0, 1))
+        pl.when(i == 0)(lambda: scatter.ready((FRONT, BACK), 0))
+        pl.when(i == 1)(lambda: scatter.ready((FRONT, BACK), 1))
 
     x[...] = acc[...].astype(BF16)
     stages[0] = gsm[...]
     sums = SmallSum(place, stages, small_box, small_send, small_recv)
     sums.start(0)
-    scatter.add_near(1)
-    scatter.add_far(0)
+    scatter.add_near(UP)
+    scatter.add_far(FRONT)
+    scatter.add_far(BACK)
     tokens.spread(3, x, gtok)
     sums.step(0)
-    scatter.add_last(2)
+    scatter.line_last(DOWN)
     sums.step(1)
-    scatter.add_near(0)
+    scatter.add_near(FRONT)
     sums.step(2)
-    scatter.add_last(1)
+    scatter.add_near(BACK)
+    scatter.add_last(UP)
     sums.finish(small)
-    scatter.add_last(0)
+    scatter.add_last(FRONT)
+    scatter.add_last(BACK)
     for i in (2, 3):
         tokens.wait(i, x_in.at[0])
-    scatter.finish()
-
-
-def layer_call(dp_count, tokens, grad_out, own, small, length):
+    scatter.finish((DOWN, UP, FRONT, BACK))
+
+
+def layer_call(dp_count, tokens, grad_out, weights, vectors, bias, lengths):
     part, width = tokens.shape[1], tokens.shape[2]
     seq = tokens.shape[0] * part
     shapes = (((4, part, width), BF16), ((4, part, width), BF16), ((3, 96, width), F32), ((16, width), F32))
@@ -648,27 +800,28 @@
     return pl.pallas_call(
         functools.partial(layer_kernel, dp_count),
         out_shape=[jax.ShapeDtypeStruct(s, d) for s, d in shapes],
-        in_specs=[vmem] * 4 + [smem],
+        in_specs=[vmem] * 8 + [smem],
         out_specs=[vmem] * 4,
         scratch_shapes=[
+            pltpu.VMEM((96, width), BF16), pltpu.VMEM((16, width), BF16),
             pltpu.VMEM((3, 4, width, 768), BF16), low_rows, low_rows, pltpu.VMEM((8, 16, width), BF16),
             pltpu.VMEM((16, width), F32), pltpu.VMEM((4, seq, 768), BF16), pltpu.VMEM((4, seq, 256), BF16),
             pltpu.VMEM((4, seq, 768), BF16), pltpu.VMEM((4, seq, 768), BF16), low_rows, wide_rows,
-            pltpu.VMEM((seq, 128), F32), wide_rows, pltpu.VMEM((4, seq, 128), F32), pltpu.VMEM((16, width), F32),
-            wide_rows, wide_rows, low_rows, pltpu.VMEM((2, width, seq), BF16), pltpu.VMEM((seq, 768), BF16),
+            pltpu.VMEM((seq, 128), F32), pltpu.VMEM((4, seq, 128), F32), pltpu.VMEM((16, width), F32),
+            wide_rows, wide_rows, low_rows, pltpu.VMEM((2, width, seq), BF16),
             pltpu.VMEM((seq, 256), BF16), pltpu.VMEM((seq, 640), BF16),
             pltpu.VMEM((3, 2, width, 768), BF16), pltpu.VMEM((3, 2, 4, 96, width), BF16),
             pltpu.VMEM((3, 4, 96, width), BF16), pltpu.VMEM((3, 3, 96, width), BF16),
             pltpu.VMEM((4, 16, width), F32), pltpu.VMEM((6, 16, width), F32),
             dma((3, 31)), dma((3, 32)), dma((4, 4)), dma((4, 4)), dma((4,)), dma((4,)), dma((8,)), dma((8,)),
-            dma((3, 2)), dma((3, 2)), dma((3, 8)), dma((3, 8)), dma((3, 4)), dma((3, 4)), dma((3, 3)), dma((3, 3)),
+            dma((3, 2)), dma((3, 2)), dma((4, 8)), dma((4, 8)), dma((4, 4)), dma((4, 4)), dma((4, 3)), dma((4, 3)),
             dma((6,)), dma((6,)),
         ],
         compiler_params=pltpu.CompilerParams(
             vmem_limit_bytes=VMEM_LIMIT, collective_id=0, has_side_effects=True
         ),
         name="layer",
-    )(tokens, grad_out, own, small, length)
+    )(tokens, grad_out, *weights, vectors, bias, lengths)
 
 
 def gather_groups(shard, dp_count, axis):
@@ -688,53 +841,19 @@
     return shard, lax.psum(small, "dp", axis_index_groups=groups)
 
 
-def pack_small(vectors, bias, dp_count, width):
-    group = lax.axis_index("dp") // (dp_count // 8)
-    part = vectors.shape[1]
-    rows = lax.dynamic_update_slice(jnp.zeros((8, width), BF16), vectors, (0, group * part))
-    units = lax.dynamic_update_slice(jnp.zeros((4 * width,), BF16), bias, (group * (4 * part),))
-    qb = rows[0].reshape(4, 192)
-    vb = rows[1].reshape(4, 192)
-    none = jnp.zeros((4, 128), BF16)
-    packed = jnp.concatenate([qb[:, :128], none, vb[:, :128], qb[:, 128:], none, vb[:, 128:], none], axis=1)
-    return jnp.concatenate([rows, units.reshape(4, width), packed], axis=0)
-
-
-def pack_attention(q, k, v, o):
-    return jnp.concatenate(
-        [q[:, :128], k[:, :128], v[:, :128], q[:, 128:], k[:, 128:], o[:, 128:], v[:, 128:], o[:, :128]], axis=1
-    )
-
-
 def shards(tokens, lengths, grad_out, qkv_weight, out_weight, up_weight, down_weight, vectors, hidden_bias):
     dp_count = lax.axis_size("dp")
-    dp_rank = lax.axis_index("dp")
-    tensor_rank = lax.axis_index("tensor")
-    width = tokens.shape[2]
-    part = width // dp_count
-
-    own = jnp.stack([
-        pack_attention(qkv_weight[0], qkv_weight[1], qkv_weight[2], out_weight.T), up_weight, down_weight.T
-    ])
-    own = gather_groups(own, dp_count, 1)
-    small = pack_small(gather_groups(vectors, dp_count, 1), gather_groups(hidden_bias, dp_count, 0), dp_count, width)
-    length = lax.dynamic_slice_in_dim(lengths, tensor_rank, 1).reshape(1, 1)
-    output, gtok, g, gsm = layer_call(dp_count, tokens, grad_out, own, small, length)
-    grad_tokens = gtok.astype(F32)
+    weights = [
+        gather_groups(weight, dp_count, axis)
+        for weight, axis in ((qkv_weight, 1), (out_weight, 1), (up_weight, 0), (down_weight, 1))
+    ]
+    weights[3] = weights[3].T
+    vectors = gather_groups(vectors, dp_count, 1)
+    bias = gather_groups(hidden_bias, dp_count, 0).reshape(1, -1)
+    output, gtok, g, gsm = layer_call(dp_count, tokens, grad_out, weights, vectors, bias, lengths)
     g, gsm = scatter_groups(g, gsm, dp_count)
-    a = g[0]
-    gq = jnp.concatenate([a[:, 0:128], a[:, 384:448]], axis=1)
-    gk = jnp.concatenate([a[:, 128:256], a[:, 448:512]], axis=1)
-    gv = jnp.concatenate([a[:, 256:384], a[:, 576:640]], axis=1)
-    gout = jnp.concatenate([a[:, 640:768], a[:, 512:576]], axis=1).T
-    packed = gsm[12:16]
-    row_q = jnp.concatenate([packed[:, 0:128], packed[:, 384:448]], axis=1).reshape(1, width)
-    row_v = jnp.concatenate([packed[:, 256:384], packed[:, 576:640]], axis=1).reshape(1, width)
-    rows = jnp.concatenate([row_q, row_v, gsm[2:8]], axis=0)
-    grad_vectors = lax.dynamic_slice_in_dim(rows, dp_rank * part, part, 1)
-    units = gsm[8:12].reshape(-1)
-    grad_bias = lax.dynamic_slice_in_dim(units, dp_rank * (part * 4), part * 4)
-    return output, grad_tokens, jnp.stack([gq, gk, gv]), gout, g[1], g[2].T, grad_vectors, grad_bias
+    *results, down, vec, units = finish_call(dp_count, output, gtok, g, gsm)
+    return *results, down.T, vec, units.reshape(-1)
 
 
 def solution(mesh):

time: 202 us -> 188 us (0.931)
  local copies, waits for them, and re-layouts: 12.6 us -> 5.47 us
  other arithmetic: 5.13 us -> 0.6 us
    pallas_call x1, Pallas kernels: 183 us -> 179 us  [layer_call(): pl.pallas_call(functools.partial(layer_kernel, dp_count), out_shape=[jax....]
    slice x19 -> x0, local copies, waits for them, and re-layouts: 3.1 us -> none  [the longest x1 0.76 us: shards(): packed[:, 576:640]]
    another operation x4 -> x0, other arithmetic: 2.56 us -> none  [the longest x1 1.8 us: shards(): jnp.stack([pack_attention(qkv_weight[0], qkv_weight[1], qkv_weight[2], ou...]
    unnamed x7 -> x8, local copies, waits for them, and re-layouts: 2.51 us -> 4.22 us
where the time goes in v4:
time: 188 us
  Pallas kernels  181 us (96%)
  local copies, waits for them, and re-layouts  5.47 us (3%)
    pallas_call x1, Pallas kernels, layer_call(): pl.pallas_call(functools.partial(layer_kernel, dp_count), out_shape=[jax....  179 us
    unnamed x8, local copies, waits for them, and re-layouts  4.22 us

profile of v4, /device:TPU:0, one launch (start us, length us, event | category | flops | bytes accessed | tf_op | source)
XLA Modules:
  0.0 188.0 jit_solution(12246402996387201461)
XLA Ops:
  0.6 1.2 reshape.22.bias_in
  1.9 179.4 %layer.1 = (bf16[4,128,768]{2,1,0:T(8,128)(2,1)}, bf16[4,128,768]{2,1,0:T(8,128)(2,1)}, f32[3,96,768]{2,1,0:T(8,128)}, f32[16,768]{1,0:T(8,128)}) custom-call(bf16[4,128,768]{2,1,0:T(8,128)(2,1)} %x_in.1, bf16[4,128,768]{2,1,0:T(8,128)(2,1)} %go_in.1, bf16[3,96,192]{2,1,0:T(8,128)(2,1)} %qkv_in.1, bf16[192,96]{1,0:T(8,128)(2,1)} %out_in.1, ...), custom_call_target="tpu_custom_call" | custom-call | tf_op jit(solution)/shard_map/layer/pallas_call | solution.py:800
  181.3 0.0 copy-start
  181.3 1.2 copy-done
  182.5 0.0 copy-start.1
  182.5 1.1 copy-done.1
  183.6 0.0 copy-start.2
  183.6 1.1 copy-done.2
  184.7 0.0 copy-start.3
  184.7 0.8 copy-done.3
  185.5 1.9 %finish.1 = (bf16[4,128,768]{2,1,0:T(8,128)(2,1)}, f32[4,128,768]{2,1,0:T(8,128)}, f32[3,96,192]{2,1,0:T(8,128)}, f32[192,96]{1,0:T(8,128)}, f32[96,768]{1,0:T(8...) custom-call(bf16[4,128,768]{2,1,0:T(8,128)(2,1)S(1)} %copy-done.1, ...), custom_call_target="tpu_custom_call" | custom-call | tf_op jit(solution)/shard_map/finish/pallas_call | solution.py:450
  187.4 0.6 reduce
Async XLA Ops:
  181.3 1.2 copy-start
  182.5 1.1 copy-start.1
  183.6 1.1 copy-start.2
  184.7 0.8 copy-start.3

commit v5 on v4

--- a/solution.py
+++ b/solution.py
@@ -156,6 +156,9 @@
     def __init__(self, place, g, boxes, sends, recvs, out):
         self.place, self.g, self.boxes, self.sends, self.recvs, self.out = place, g, boxes, sends, recvs, out
 
+    def swapped(self, part):
+        return self.place.c
+
     def box(self, stage, part, *index):
         return self.boxes[stage].at[(part[1], *index, slice(None), pl.ds(*part[2]))]
 
@@ -168,7 +171,7 @@
         ).start()
 
     def piece(self, part, s, f, j):
-        z, x, y = self.place.shifted(j, s, f, self.place.c)
+        z, x, y = self.place.shifted(j, s, f, self.swapped(part))
         return part[1], y * 2 + self.place.c, pl.multiple_of((z * 2 + x) * 96, 96)
 
     def wait(self, stage, part, index, sem):
@@ -191,17 +194,15 @@
 
     def across(self, part, f):
         for j in (2, 1, 3, 0):
-            self.push(1, part, f, 1, j, (f, j), 4 * f + j, self.place.second(self.place.c))
+            self.push(1, part, f, 1, j, (f, j), 4 * f + j, self.place.second(self.swapped(part)))
 
     def ready(self, parts, i):
         if i == 0:
             for part in parts:
                 self.across(part, 1)
 
-        @pl.when(self.place.c == i)
-        def _():
-            for part in parts:
-                self.across(part, 0)
+        for part in parts:
+            pl.when(self.swapped(part) == i)(lambda: self.across(part, 0))
 
     def total(self, part, f, j, views, last=False):
         k, t, row = self.piece(part, 0, f, j)
@@ -224,13 +225,13 @@
             self.wait(stage, part, index, sem)
         self.total(part, f, j, [(stage, index) for stage, index, _ in arrived], last)
 
-    def add_far(self, part):
-        for j in (2, 1, 3, 0):
+    def add_far(self, part, line=(2, 1, 3, 0)):
+        for j in line:
             self.add(part, 1, j, [(1, (1, j), 4 + j)])
-            self.push(2, part, 1, 0, j, (j,), j, self.place.first(self.place.c))
-
-    def add_near(self, part):
-        for j in (2, 1, 3):
+            self.push(2, part, 1, 0, j, (j,), j, self.place.first(self.swapped(part)))
+
+    def add_near(self, part, line=(2, 1, 3)):
+        for j in line:
             self.add(part, 0, j, [(1, (0, j), j), (2, (j,), j)])
             self.push(3, part, 0, 0, j, (3 - j,), 3 - j, self.place.along(j))
 
@@ -238,19 +239,19 @@
         arrived = [(1, (0, 0), 0), (2, (0,), 0), (3, (0,), 0), (3, (1,), 1), (3, (2,), 2)]
         self.add(part, 0, 0, arrived, True)
 
-    def line_far(self, part):
-        for j in (2, 1, 3):
+    def line_far(self, part, line=(2, 1, 3)):
+        for j in line:
             self.add(part, 1, j, [(1, (1, j), 4 + j)])
             self.push(2, part, 1, 0, j, (3 - j,), 3 - j, self.place.along(j))
 
-    def line_near(self, part):
-        for j in (2, 1, 3):
+    def line_near(self, part, line=(2, 1, 3)):
+        for j in line:
             self.add(part, 0, j, [(1, (0, j), j)])
             self.push(3, part, 0, 0, j, (3 - j,), 3 - j, self.place.along(j))
 
     def line_turn(self, part):
         self.add(part, 1, 0, [(1, (1, 0), 4), (2, (0,), 0), (2, (1,), 1), (2, (2,), 2)])
-        self.push(2, part, 1, 0, 0, (3,), 3, self.place.first(self.place.c))
+        self.push(2, part, 1, 0, 0, (3,), 3, self.place.first(self.swapped(part)))
 
     def line_last(self, part):
         arrived = [(1, (0, 0), 0), (3, (0,), 0), (3, (1,), 1), (3, (2,), 2), (2, (3,), 3)]
@@ -365,6 +366,26 @@
 DOWN, UP, FRONT, BACK = (2, 2, (0, 768)), (1, 1, (0, 768)), (0, 0, (0, 512)), (3, 0, (512, 256))
 
 
+def sums_in_up(scatter):
+    return (
+        ((1, scatter.line_far, DOWN),),
+        ((1, scatter.line_near, DOWN, (2, 1)),),
+    )
+
+
+def sums_in_attention(scatter):
+    return (
+        ((0, scatter.line_near, DOWN, (3,)), (0, scatter.add_far, UP, (2,)), (1, scatter.add_near, UP, (2,))),
+        ((0, scatter.add_far, UP, (1,)), (1, scatter.add_near, UP, (1,))),
+        ((0, scatter.add_far, UP, (3,)), (1, scatter.add_near, UP, (3,))),
+        ((0, scatter.add_far, UP, (0,)),),
+        (),
+        ((0, scatter.line_turn, DOWN),),
+        (),
+        (),
+    )
+
+
 def spots(rows, offset, gap=0):
     source = lax.broadcasted_iota(jnp.int32, (96, 768), 0) + rows
     target = lax.broadcasted_iota(jnp.int32, (96, 768), 1)
@@ -379,7 +400,7 @@
     start = 96 * (group % 2)
     queries = dot(rows, spots(start, 0, 256))[0:1]
     values = dot(rows, spots(start, 256, 192))[1:2]
-    units = bias_in[...].astype(F32)
+    units = bias_in[...].astype(F32).reshape(1, bias_in.shape[0])
     lane = lax.broadcasted_iota(jnp.int32, (1, 768), 1)
     units = jnp.where(lane // 384 == group % 2, jnp.concatenate([units, units], axis=1), 0.0)
     line = lax.broadcasted_iota(jnp.int32, (8, 768), 0)
@@ -437,14 +458,14 @@
     vec[...] = lines[:, 0:part]
     row = jnp.sum(jnp.where(line == group // 2, packed, 0.0), axis=0, keepdims=True)
     shift = 384 * (group % 2) + rest * 4 * part
-    units[...] = pltpu.roll(row, (768 - shift) % 768, 1)[:, 0 : 4 * part]
+    units[...] = pltpu.roll(row, (768 - shift) % 768, 1)[:, 0 : 4 * part].reshape(4 * part)
 
 
 def finish_call(dp_count, out, gtok, shard, small):
     rows, width = shard.shape[1], shard.shape[2]
     shapes = (
         (out.shape, BF16), (gtok.shape, F32), ((3, rows, width // 4), F32), ((width // 4, rows), F32),
-        ((rows, width), F32), ((rows, width), F32), ((8, rows), F32), ((1, 4 * rows), F32),
+        ((rows, width), F32), ((rows, width), F32), ((8, rows), F32), ((4 * rows,), F32),
     )
     vmem = pl.BlockSpec(memory_space=pltpu.VMEM)
     return pl.pallas_call(
@@ -452,7 +473,7 @@
         out_shape=[jax.ShapeDtypeStruct(s, d) for s, d in shapes],
         in_specs=[vmem] * 4,
         out_specs=[vmem] * 8,
-        compiler_params=pltpu.CompilerParams(vmem_limit_bytes=32 * 1024 * 1024),
+        compiler_params=pltpu.CompilerParams(vmem_limit_bytes=VMEM_LIMIT),
         name="finish",
     )(out, gtok, shard, small)
 
@@ -661,17 +682,27 @@
         acc[...] += dot_nt(gp[t], w[1, t])
         return dot(tall[1], gp[t])
 
+    def sums_at(i, events):
+        for turn in (0, 1):
+            now = [event for event in events if event[0] == turn]
+            if now:
+                @pl.when(i == turn)
+                def _():
+                    for _, function, *arguments in now:
+                        function(*arguments)
+
     for k, back in ((2, down_back), (1, up_back)):
+        events = ((), ()) if k == 2 else sums_in_up(scatter)
+
         @pl.loop(0, 2)
         def _(i):
             t = chunk(i, 1 - place.c)
             w[k, t] = back(t).astype(BF16)
             scatter.to_partner(k, t, i)
-
-        @pl.loop(0, 2)
-        def _(i):
+            sums_at(i, events[0])
             t = chunk(i, place.c)
             own_chunk(k, i, t, back(t))
+            sums_at(i, events[1])
 
     @pl.loop(0, blocks)
     def _(r):
@@ -722,6 +753,7 @@
             part = (0, HD, HD)[h]
             keys_tall = jnp.transpose(keys.astype(F32))[part : part + HD, :].astype(BF16)
             grads_q.append(dot(keys_tall, grad_scores) * 0.125)
+            event(h)
         pair = jnp.transpose(jnp.concatenate([grads_q[0], grads_q[1]], axis=0))
         single = jnp.transpose(jnp.concatenate([grads_q[2], jnp.zeros_like(grads_q[2])], axis=0))
         tiles = [pair, grads_k[0] + grads_k[1], grads_v[0] + grads_v[1], single + grads_k[2], grads_v[2]]
@@ -729,7 +761,7 @@
             span = slice(128 * i, 128 * i + 128)
             put_row(gsm, 4 + t, span, jnp.sum(tile, axis=0, keepdims=True))
             gpacked[:, span] = tile.astype(BF16)
-        event()
+        event(3)
         acc[...] += dot_nt(gpacked[...], w[0, t, :, 0:640])
         store(slice(0, 512), dot(tall[1], gpacked[:, 0:512]))
         store(slice(512, 640), dot(tall[1], gpacked[:, 512:640]) + dot(tall[0], ctx[t, :, 0:128]))
@@ -737,31 +769,28 @@
 
     @pl.loop(0, 2)
     def _(i):
-        t = chunk(i, 1 - place.c)
-
-        def store(span, value):
-            w[0, t, :, span] = value.astype(BF16)
-
-        def event():
-            pl.when(i == 0)(lambda: scatter.line_far(DOWN))
-            pl.when(i == 1)(lambda: scatter.line_near(DOWN))
-
-        attention_back(t, event, store)
-        scatter.to_partner(0, t, i)
-
-    @pl.loop(0, 2)
-    def _(i):
-        t = chunk(i, place.c)
-
-        def store(span, value):
-            w[0, t, :, span] = (value + box_p[0, i, :, span].astype(F32)).astype(BF16)
-
-        def event():
-            pl.when(i == 0)(lambda: scatter.add_far(UP))
-            pl.when(i == 1)(lambda: scatter.line_turn(DOWN))
-            scatter.from_partner(0, i)
-
-        attention_back(t, event, store)
+        other = chunk(i, 1 - place.c)
+        mine = chunk(i, place.c)
+
+        def store_other(span, value):
+            w[0, other, :, span] = value.astype(BF16)
+
+        def store_mine(span, value):
+            w[0, mine, :, span] = (value + box_p[0, i, :, span].astype(F32)).astype(BF16)
+
+        events = sums_in_attention(scatter)
+
+        def event_other(h):
+            sums_at(i, events[h])
+
+        def event_mine(h):
+            sums_at(i, events[4 + h])
+            if h == 3:
+                scatter.from_partner(0, i)
+
+        attention_back(other, event_other, store_other)
+        scatter.to_partner(0, other, i)
+        attention_back(mine, event_mine, store_mine)
         pl.when(i == 0)(lambda: scatter.ready((FRONT, BACK), 0))
         pl.when(i == 1)(lambda: scatter.ready((FRONT, BACK), 1))
 
@@ -769,16 +798,15 @@
     stages[0] = gsm[...]
     sums = SmallSum(place, stages, small_box, small_send, small_recv)
     sums.start(0)
-    scatter.add_near(UP)
     scatter.add_far(FRONT)
     scatter.add_far(BACK)
     tokens.spread(3, x, gtok)
     sums.step(0)
+    scatter.add_near(FRONT)
+    sums.step(1)
+    scatter.add_near(BACK)
+    sums.step(2)
     scatter.line_last(DOWN)
-    sums.step(1)
-    scatter.add_near(FRONT)
-    sums.step(2)
-    scatter.add_near(BACK)
     scatter.add_last(UP)
     sums.finish(small)
     scatter.add_last(FRONT)
@@ -849,11 +877,11 @@
     ]
     weights[3] = weights[3].T
     vectors = gather_groups(vectors, dp_count, 1)
-    bias = gather_groups(hidden_bias, dp_count, 0).reshape(1, -1)
+    bias = gather_groups(hidden_bias, dp_count, 0)
     output, gtok, g, gsm = layer_call(dp_count, tokens, grad_out, weights, vectors, bias, lengths)
     g, gsm = scatter_groups(g, gsm, dp_count)
     *results, down, vec, units = finish_call(dp_count, output, gtok, g, gsm)
-    return *results, down.T, vec, units.reshape(-1)
+    return *results, down.T, vec, units
 
 
 def solution(mesh):

time: 188 us -> 180 us (0.957)
  local copies, waits for them, and re-layouts: 5.47 us -> 0 us
  Pallas kernels: 181 us -> 179 us
    unnamed x8 -> x0, local copies, waits for them, and re-layouts: 4.22 us -> none
    pallas_call x1, Pallas kernels: 179 us -> 175 us  [layer_call(): pl.pallas_call(functools.partial(layer_kernel, dp_count), out_shape=[jax....]
where the time goes in v5:
time: 180 us; the launch traced here: 179 us
  Pallas kernels  179 us (99%)
    pallas_call x1, Pallas kernels, layer_call(): pl.pallas_call(functools.partial(layer_kernel, dp_count), out_shape=[jax....  175 us

profile of v5, /device:TPU:0, one launch (start us, length us, event | category | flops | bytes accessed | tf_op | source)
XLA Modules:
  0.0 179.4 jit_solution(786268083326314035)
XLA Ops:
  0.6 175.3 %layer.1 = (bf16[4,128,768]{2,1,0:T(8,128)(2,1)}, bf16[4,128,768]{2,1,0:T(8,128)(2,1)}, f32[3,96,768]{2,1,0:T(8,128)}, f32[16,768]{1,0:T(8,128)}) custom-call(bf16[4,128,768]{2,1,0:T(8,128)(2,1)} %x_in.1, bf16[4,128,768]{2,1,0:T(8,128)(2,1)} %go_in.1, bf16[3,96,192]{2,1,0:T(8,128)(2,1)} %qkv_in.1, bf16[192,96]{1,0:T(8,128)(2,1)} %out_in.1, ...), custom_call_target="tpu_custom_call" | custom-call | tf_op jit(solution)/shard_map/layer/pallas_call | solution.py:828
  175.9 3.5 %finish.1 = (bf16[4,128,768]{2,1,0:T(8,128)(2,1)}, f32[4,128,768]{2,1,0:T(8,128)}, f32[3,96,192]{2,1,0:T(8,128)}, f32[192,96]{1,0:T(8,128)}, f32[96,768]{1,0:T(8...) custom-call(bf16[4,128,768]{2,1,0:T(8,128)(2,1)} %get-tuple-element.20.out_in, ...), custom_call_target="tpu_custom_call" | custom-call | tf_op jit(solution)/shard_map/finish/pallas_call | solution.py:471

commit v6 on v5

--- a/solution.py
+++ b/solution.py
@@ -134,9 +134,7 @@
     def relay(self, k, s, f, order):
         for j in order:
             self.wait(k, 8 * s + 4 * f + j)
-            if k == 2 and (s, f, j) == (0, 1, 0):
-                self.along(k, 1)
-            self.forward(k, s, f, j, "p" if s else "sp" if f or k == 2 else "fsp")
+            self.forward(k, s, f, j, "p" if s else "sp" if f else "fsp")
 
     def others(self, k):
         @pl.loop(16, 32)
@@ -615,9 +613,9 @@
             act[t, rows, :] = (u * cdf).astype(BF16)
             gp[t, rows, :] = (cdf + u * density).astype(BF16)
 
+    tokens.gather(1, go_in, go)
     for event in LATE:
         gather.relay(*event)
-    tokens.gather(1, go_in, go)
     gather.others(2)
 
     @pl.loop(0, 4)

time: 180 us -> 176 us (0.978)
  Pallas kernels: 179 us -> 176 us
    pallas_call x1, Pallas kernels: 175 us -> 172 us  [layer_call(): pl.pallas_call(functools.partial(layer_kernel, dp_count), out_shape=[jax....]
where the time goes in v6:
time: 176 us
  Pallas kernels  176 us (100%)
    pallas_call x1, Pallas kernels, layer_call(): pl.pallas_call(functools.partial(layer_kernel, dp_count), out_shape=[jax....  172 us
    pallas_call x1, Pallas kernels, finish_call(): pl.pallas_call(functools.partial(finish_kernel, dp_count), out_shape=[jax...  3.53 us

profile of v6, /device:TPU:0, one launch (start us, length us, event | category | flops | bytes accessed | tf_op | source)
XLA Modules:
  0.0 176.2 jit_solution(9272147834250305984)
XLA Ops:
  0.6 172.0 %layer.1 = (bf16[4,128,768]{2,1,0:T(8,128)(2,1)}, bf16[4,128,768]{2,1,0:T(8,128)(2,1)}, f32[3,96,768]{2,1,0:T(8,128)}, f32[16,768]{1,0:T(8,128)}) custom-call(bf16[4,128,768]{2,1,0:T(8,128)(2,1)} %x_in.1, bf16[4,128,768]{2,1,0:T(8,128)(2,1)} %go_in.1, bf16[3,96,192]{2,1,0:T(8,128)(2,1)} %qkv_in.1, bf16[192,96]{1,0:T(8,128)(2,1)} %out_in.1, ...), custom_call_target="tpu_custom_call" | custom-call | tf_op jit(solution)/shard_map/layer/pallas_call | solution.py:826
  172.7 3.5 %finish.1 = (bf16[4,128,768]{2,1,0:T(8,128)(2,1)}, f32[4,128,768]{2,1,0:T(8,128)}, f32[3,96,192]{2,1,0:T(8,128)}, f32[192,96]{1,0:T(8,128)}, f32[96,768]{1,0:T(8...) custom-call(bf16[4,128,768]{2,1,0:T(8,128)(2,1)} %get-tuple-element.20.out_in, ...), custom_call_target="tpu_custom_call" | custom-call | tf_op jit(solution)/shard_map/finish/pallas_call | solution.py:469
